TPU v7x, 32 devices: a whole 2x2x4 slice. The times are simulated.
32 devices in a mesh: video: 2 (over y), block: 4 (over z), band: 2 (over x), chan: 2 (over core).
Axes of the slice: x: 2, y: 2, z: 4, core: 2. Of those that a mesh axis runs over, the one named last changes fastest.
Arguments:
- latents: bfloat16 [32, 2, 1664], P(('video', 'block'), 'band'), parts along dimension 0, may hold values from -60 to 60
- frame_counts: int32 [8], P('video'), parts along dimension 0, may hold values from 1 to 4, 8 in all
- w_in: bfloat16 [3, 3, 3, 16, 384], replicated, may hold values from -0.3125 to 0.3125
- gain_in: float32 [384], replicated, may hold values from 0.1 to 1.9
- shift_in: float32 [384], replicated, may hold values from -3 to 3
- w_mid: bfloat16 [3, 3, 3, 384, 384], P(None, None, None, None, 'chan'), may hold values from -0.0625 to 0.0625
- gain_out: float32 [384], P('chan'), may hold values from 0.1 to 1.9
- shift_out: float32 [384], P('chan'), may hold values from -3 to 3
Outputs:
- decoded: bfloat16 [32, 2, 104, 384], P(('video', 'block'), 'band', None, 'chan'), parts along dimension 0
There are 2 independent parts, one for each index of `video`. A program takes and returns all parts, laid end to end along the dimension named above; an argument that names none is the same for every part. Nothing has to cross between parts.
Inputs may be any that keep to these rules, and one draw needn't show every extreme that they name: `frame_counts`: entry k is the number of consecutive latent frames that device k of the frame axis holds; the entries sum to 8.
All inputs are finite; a program needn't handle non-finite values.
Results may differ from a plain program's by a relative error of at most 0.013.
Values may be sent and summed in bfloat16 or wider, within the bound.
No kernel may reach another device: no remote copies, remote signals or barrier semaphores. Data moves between devices by JAX's collectives and lax.ppermute only.
A program may use at most 64 MiB of HBM per device.

v0:
```python
import jax
import jax.numpy as jnp
from jax import lax
from jax.sharding import PartitionSpec as P

LAT = 16
C = 384
GROUPS = 32


EPSILON = 1e-06


def with_halo(cells, sides, width):
    for axis, dim in sides:
        count = lax.axis_size(axis)
        ends = count - 1
        head = lax.slice_in_dim(cells, 0, width, axis=dim)
        tail = lax.slice_in_dim(cells, cells.shape[dim] - width, cells.shape[dim], axis=dim)
        cells = jnp.concatenate(
            [
                lax.ppermute(tail, axis, [(i, (i + 1) % count) for i in range(ends)]),
                cells,
                lax.ppermute(head, axis, [((i + 1) % count, i) for i in range(ends)]),
            ],
            axis=dim,
        )
    return cells


def count_for(frame_counts, position):
    places = jnp.arange(frame_counts.shape[0], dtype=jnp.int32)
    return jnp.sum(jnp.where(places == position, frame_counts, 0))


def start_for(frame_counts, position):
    places = jnp.arange(frame_counts.shape[0], dtype=jnp.int32)
    return jnp.sum(jnp.where(places < position, frame_counts, 0))


def rows_beside(values):
    return with_halo(values, (("band", 1),), 1)


def group_silu(values, norm_gain, norm_shift):
    in_frames, band_rows, columns, local_width = values.shape
    group_width = C // GROUPS
    local_groups = local_width // group_width
    grouped = values.reshape(in_frames, band_rows * columns, local_groups, group_width)
    group_total, squares = lax.psum(
        (jnp.sum(grouped, axis=(1, 3)), jnp.sum(grouped * grouped, axis=(1, 3))), "band"
    )
    total = float(lax.axis_size("band") * band_rows * columns * group_width)
    group_mean = group_total / total
    variance = squares / total - group_mean * group_mean
    inverse = lax.rsqrt(variance + EPSILON)
    normed = (grouped - group_mean[:, None, :, None]) * inverse[:, None, :, None]
    normed = normed.reshape(values.shape)
    return jax.nn.silu(normed * norm_gain + norm_shift)


def latent_conv(extended, kernel):
    steps_in, rows_padded, flat_width = extended.shape
    lat_width = kernel.shape[3]
    out_width = kernel.shape[4]
    columns = flat_width // lat_width
    out_frames = steps_in - 2
    band_rows = rows_padded - 2
    latent_grid = extended.reshape(steps_in, rows_padded, columns, lat_width)
    latent_grid = jnp.pad(latent_grid, ((0, 0), (0, 0), (1, 1), (0, 0)))
    patches = []
    for step_t in range(3):
        for step_y in range(3):
            for step_x in range(3):
                patches.append(
                    latent_grid[
                        step_t : step_t + out_frames,
                        step_y : step_y + band_rows,
                        step_x : step_x + columns,
                        :,
                    ]
                )
    stacked = jnp.concatenate(patches, axis=-1).reshape(-1, 27 * lat_width)
    result = jnp.dot(
        stacked, kernel.reshape(27 * lat_width, out_width), preferred_element_type=jnp.float32
    )
    return result.reshape(out_frames, band_rows, columns, out_width)


def weighted_taps(padded, kernel):
    in_frames, rows_padded, cols_padded, in_width = padded.shape
    out_frames = in_frames - 2
    band_rows = rows_padded - 2
    columns = cols_padded - 2
    out_width = kernel.shape[4]
    accumulate = jnp.zeros((out_frames * band_rows * columns, out_width), jnp.float32)
    for step_t in range(3):
        for step_y in range(3):
            patches = [
                padded[
                    step_t : step_t + out_frames,
                    step_y : step_y + band_rows,
                    step_x : step_x + columns,
                    :,
                ]
                for step_x in range(3)
            ]
            stacked = jnp.concatenate(patches, axis=-1).reshape(-1, 3 * in_width)
            accumulate = accumulate + jnp.dot(
                stacked,
                kernel[step_t, step_y].reshape(3 * in_width, out_width),
                preferred_element_type=jnp.float32,
            )
    return accumulate.reshape(out_frames, band_rows, columns, out_width)


def middle_section(act_extended, w_mid, gain_out, shift_out):
    padded = jnp.pad(rows_beside(act_extended), ((0, 0), (0, 0), (1, 1), (0, 0)))
    second_conv = weighted_taps(lax.all_gather(padded, "chan", axis=3, tiled=True), w_mid)
    second_conv = second_conv.astype(jnp.bfloat16)
    return group_silu(second_conv.astype(jnp.float32), gain_out, shift_out).astype(jnp.bfloat16)


def shards(latents, frame_counts, w_in, gain_in, shift_in, w_mid, gain_out, shift_out):
    frames, band_rows, flat_width = latents.shape
    columns = flat_width // LAT
    half_width = w_mid.shape[4]
    position = lax.axis_index("block")
    live_count = count_for(frame_counts, position)
    offset = lax.axis_index("chan") * half_width
    front_kernel = lax.dynamic_slice_in_dim(w_in, offset, half_width, 4)
    front_gain = lax.dynamic_slice_in_dim(gain_in, offset, half_width, 0)
    front_shift = lax.dynamic_slice_in_dim(shift_in, offset, half_width, 0)
    share = frames // 2
    all_slots = lax.all_gather(latents, "block", axis=0, tiled=True)
    run_ends = jnp.cumsum(frame_counts)
    run_starts = run_ends - frame_counts
    first_frame = position * share - 4
    wanted = first_frame + jnp.arange(share + 4, dtype=jnp.int32)
    owners = jnp.sum((wanted[:, None] >= run_ends[None, :]).astype(jnp.int32), axis=1)
    slot_ids = owners * frames + wanted - jnp.take(run_starts, owners)
    slot_ids = jnp.clip(slot_ids, 0, all_slots.shape[0] - 1)
    picked = jnp.take(all_slots, slot_ids, axis=0)
    latent_extended = jnp.where((wanted >= 0)[:, None, None], picked, jnp.zeros_like(picked))
    first_conv = latent_conv(rows_beside(latent_extended), front_kernel).astype(jnp.bfloat16)
    activated = group_silu(first_conv.astype(jnp.float32), front_gain, front_shift).astype(
        jnp.bfloat16
    )
    act_ids = first_frame + 2 + jnp.arange(share + 2, dtype=jnp.int32)
    act_extended = jnp.where(
        (act_ids >= 0)[:, None, None, None], activated, jnp.zeros_like(activated)
    )
    even_norm = middle_section(act_extended, w_mid, gain_out, shift_out)
    my_start = start_for(frame_counts, position)
    slot_places = jnp.arange(frames, dtype=jnp.int32)
    slot_frames = my_start + slot_places
    slot_alive = slot_places < live_count
    initial = jnp.zeros((frames, band_rows, columns, half_width), jnp.bfloat16)
    piece = lax.all_gather(even_norm, "block", axis=0, tiled=True)
    valid = (slot_frames >= 0) & (slot_frames < piece.shape[0]) & slot_alive
    took = jnp.take(piece, jnp.clip(slot_frames, 0, piece.shape[0] - 1), axis=0)
    return jnp.where(valid[:, None, None, None], took, initial)


def solution(mesh):
    return jax.shard_map(
        shards,
        mesh=mesh,
        in_specs=(
            P(("video", "block"), "band", None),
            P("video"),
            P(),
            P(),
            P(),
            P(None, None, None, None, "chan"),
            P("chan"),
            P("chan"),
        ),
        out_specs=P(("video", "block"), "band", None, "chan"),
        check_vma=False,
    )
```

profile of v0, /device:TPU:0, one launch (start us, length us, event | category | flops | bytes accessed | tf_op | source)
XLA Modules:
  0.0 121.1 jit_solution(8071006151488944462)
XLA Ops:
  0.0 0.9 reduce-window.8
  0.9 1.3 %fusion.23 = (s32[]{:T(128)}, s32[]{:T(128)}, s32[4]{0:T(128)S(1)}) fusion(s32[4]{0:T(128)} %param.9, s32[]{:T(128)S(6)} %axis_index.23, s32[4,1]{0,1:T(1,128)S(1)} %reduce-window.8), kind=kLoop, calls=%fused_computation.78 | loop fusion | flops 26 | bytes 60 | tf_op jit(solution)/shard_map/reduce_sum | solution.py:33
  3.0 0.7 copy.111
  3.7 15.1 %all_gather.9 = bf16[16,1,1664]{2,1,0:T(2,128)(2,1)S(1)} all-gather(bf16[4,1,1664]{2,1,0:T(2,128)(2,1)S(1)} %copy.111), channel_id=1, replica_groups=mesh['video'=2,'block'=4,'band'=2,'chan'=2] {'block'}, dimensions={0}, use_global_device_ids=true | all-gather | bytes 66560 | tf_op jit(solution)/shard_map/all_gather | solution.py:135
  19.5 1.3 %collective-permute-start.1 = (bf16[6,1,1664]{2,0,1:T(8,128)(2,1)S(1)}, bf16[6,1,1664]{2,0,1:T(8,128)(2,1)S(1)}, u32[]{:S(2)}, u32[]{:S(2)}) collective-permute-start(bf16[6,1,1664]{2,0,1:T(8,128)(2,1)S(1)} %fusion.21), channel_id=1, source_target_pairs={{2,0},{3,1},{6,4},{7,5},{10,8},{11,9},{14,12},{15,13},{18,16},{19,... | collective-permute-start | bytes 59912 | tf_op jit(solution)/shard_map/ppermute | solution.py:24
  20.8 4.5 %collective-permute-start = (bf16[6,1,1664]{2,0,1:T(8,128)(2,1)S(1)}, bf16[6,1,1664]{2,0,1:T(8,128)(2,1)S(1)}, u32[]{:S(2)}, u32[]{:S(2)}) collective-permute-start(bf16[6,1,1664]{2,0,1:T(8,128)(2,1)S(1)} %fusion.21), channel_id=1, source_target_pairs={{0,2},{1,3},{4,6},{5,7},{8,10},{9,11},{12,14},{13,15},{16,18},{17,... | collective-permute-start | bytes 59912 | tf_op jit(solution)/shard_map/ppermute | solution.py:22
  25.6 0.8 fusion.36
  26.4 3.6 %fusion.32 = (bf16[1,1,3,384,192]{3,4,2,1,0:T(8,128)(2,1)S(1)}, bf16[1,1,3,384,192]{3,4,2,1,0:T(8,128)(2,1)S(1)}, bf16[1,1,3,384,192]{3,4,2,1,0:T(8,128)(2,1)S(1...) fusion(bf16[3,3,3,384,192]{3,4,2,1,0:T(8,128)(2,1)} %param.13), kind=kLoop, calls=%fused_computation.95 | loop fusion | bytes 7962624 | tf_op jit(solution)/shard_map/slice | solution.py:111
  29.9 0.8 constant_dynamic-slice_fusion
  30.8 1.8 %compare_and_fusion.1 = (pred[4]{0:T(512)(128)(4,1)}, pred[4]{0:T(512)(128)(4,1)}) fusion(s32[]{:T(128)} %get-tuple-element.10, s32[]{:T(128)} %get-tuple-element.9), kind=kLoop, calls=%fused_computation.71 | loop fusion | flops 52 | bytes 16 | tf_op jit(solution)/shard_map/jit(_take)/and | solution.py:161
  33.2 0.7 dynamic_slice.11
  35.1 1.3 %fusion.35 = (bf16[4,1,104,16]{3,2,0,1:T(8,128)(2,1)}, bf16[4,1,104,16]{3,2,0,1:T(8,128)(2,1)}, bf16[4,1,104,16]{3,2,0,1:T(8,128)(2,1)}, bf16[4,1,104,16]{3,2,0,...) fusion(bf16[6,3,106,16]{3,2,0,1:T(8,128)(2,1)S(1)} %fusion.14), kind=kLoop, calls=%fused_computation.98 | loop fusion | bytes 479232 | tf_op jit(solution)/shard_map/slice | solution.py:76
  37.2 0.8 slice.234
  38.0 0.8 slice.238
  38.8 1.5 %slice.245 = bf16[4,1,104,16]{3,2,0,1:T(8,128)(2,1)} reshape(bf16[4,1,1664]{2,0,1:T(4,128)(2,1)} %get-tuple-element.73) | data formatting | bytes 26624 | tf_op jit(solution)/shard_map/slice | solution.py:76
  40.3 0.8 slice.249
  41.1 1.5 %slice.256 = bf16[4,1,104,16]{3,2,0,1:T(8,128)(2,1)} reshape(bf16[4,1,1664]{2,0,1:T(4,128)(2,1)} %get-tuple-element.72) | data formatting | bytes 26624 | tf_op jit(solution)/shard_map/slice | solution.py:76
  42.6 4.0 %concatenate.44 = bf16[4,1,104,432]{3,2,0,1:T(8,128)(2,1)} concatenate(bf16[4,1,104,16]{3,2,0,1:T(8,128)(2,1)} %get-tuple-element.68, bf16[4,1,104,16]{3,2,0,1:T(8,128)(2,1)S(1)} %slice.227, bf16[4,1,104,16]{3,2,0,1:T(8,128)(2,1)} %get-tuple-element.67, bf16[4,1,104,16]{3,2,0,1:T(8,128)(2,1)} %get-tuple-element.66, bf16[4,1,104,16]{3,2,0,1:T(8,128)(2,1)S(1)} %copy-done.18, ...), dimensions={3} | concatenate | bytes 718848 | tf_op jit(solution)/shard_map/concatenate | solution.py:83
  46.6 2.2 %fusion.30 = (f32[4,192]{1,0:T(4,128)S(1)}, f32[4,192]{1,0:T(4,128)S(1)}, f32[4,104,192]{1,2,0:T(8,128)}) fusion(bf16[432,192,1]{1,0,2:T(8,128)(2,1)} %bitcast.174, bf16[4,1,104,432]{3,2,0,1:T(8,128)(2,1)} %concatenate.44), kind=kOutput, calls=%fused_computation.93 | convolution fusion | flops 69407232 | bytes 850944 | tf_op jit(solution)/shard_map/dot_general | solution.py:84
  49.1 4.9 %all-reduce.3 = (f32[4,16]{1,0:T(4,128)S(1)}, f32[4,16]{1,0:T(4,128)S(1)}) all-reduce(f32[4,16]{1,0:T(4,128)S(1)} %reduce_sum.88, f32[4,16]{1,0:T(4,128)S(1)} %reduce_sum.85), channel_id=1, replica_groups=mesh['video'=2,'block'=4,'band'=2,'chan'=2] {'band'}, use_global_device_ids=true, to_apply=%region_9.10 | all-reduce | flops 128 | bytes 1024 | tf_op jit(solution)/shard_map/psum | solution.py:50
  54.4 1.3 %select_bitcast_fusion = bf16[4,1,104,192]{2,3,0,1:T(8,128)(2,1)S(1)} fusion(f32[192]{0:T(256)S(1)} %copy-done.19, f32[192]{0:T(256)S(1)} %copy-done.20, f32[4,192]{1,0:T(4,128)S(1)} %mul.122, f32[4,104,192]{1,2,0:T(8,128)} %get-tuple-element.83, f32[4,192]{1,0:T(4,128)S(1)} %sub.66, pred[4]{0:T(512)(128)(4,1)S(1)} %copy-done.27), kind=kLoop, calls=%fused_computation.52 | loop fusion | flops 798720 | bytes 486916 | tf_op jit(solution)/shard_map/jit(_where)/select_n | solution.py:150
  55.8 1.3 %collective-permute-start.3 = (bf16[4,1,104,192]{2,3,0,1:T(8,128)(2,1)S(1)}, bf16[4,1,104,192]{2,3,0,1:T(8,128)(2,1)S(1)}, u32[]{:S(2)}, u32[]{:S(2)}) collective-permute-start(bf16[4,1,104,192]{2,3,0,1:T(8,128)(2,1)S(1)} %select_bitcast_fusion), channel_id=1, source_target_pairs={{2,0},{3,1},{6,4},{7,5},{10,8},{11,9},{14,12},{15,13},{18,16},{19,... | collective-permute-start | bytes 479240 | tf_op jit(solution)/shard_map/ppermute | solution.py:24
  57.1 4.6 %collective-permute-start.2 = (bf16[4,1,104,192]{2,3,0,1:T(8,128)(2,1)S(1)}, bf16[4,1,104,192]{2,3,0,1:T(8,128)(2,1)S(1)}, u32[]{:S(2)}, u32[]{:S(2)}) collective-permute-start(bf16[4,1,104,192]{2,3,0,1:T(8,128)(2,1)S(1)} %select_bitcast_fusion), channel_id=1, source_target_pairs={{0,2},{1,3},{4,6},{5,7},{8,10},{9,11},{12,14},{13,15},{16,18},{17,... | collective-permute-start | bytes 479240 | tf_op jit(solution)/shard_map/ppermute | solution.py:22
  62.7 0.8 copy.138
  64.2 0.8 copy.139
  65.7 0.8 copy.140
  67.0 0.8 copy.141
  68.2 0.8 copy.142
  69.4 0.8 copy.143
  70.6 0.8 copy.144
  71.8 0.8 copy.145
  73.0 0.8 copy.146
  74.2 2.8 %all_gather.10 = bf16[4,3,106,384]{2,3,0,1:T(8,128)(2,1)S(1)} all-gather(bf16[4,3,106,192]{2,3,0,1:T(8,128)(2,1)S(1)} %fusion.12), channel_id=1, replica_groups=mesh['video'=2,'block'=4,'band'=2,'chan'=2] {'chan'}, dimensions={3}, use_global_device_ids=true | all-gather | bytes 1465344 | tf_op jit(solution)/shard_map/all_gather | solution.py:119
  77.4 2.3 %fusion.33 = (bf16[2,1,104,384]{2,3,0,1:T(8,128)(2,1)S(1)}, bf16[2,1,104,384]{2,3,0,1:T(8,128)(2,1)}, bf16[2,1,104,384]{2,3,0,1:T(8,128)(2,1)}, bf16[2,1,104,384...) fusion(bf16[4,3,106,384]{2,3,0,1:T(8,128)(2,1)S(1)} %all_gather.10), kind=kLoop, calls=%fused_computation.96 | loop fusion | bytes 6070272 | tf_op jit(solution)/shard_map/slice | solution.py:100
  79.8 1.0 copy.113
  82.3 1.1 pad_maximum_fusion.3
  83.7 1.0 pad_maximum_fusion.4
  85.1 1.2 %pad_maximum_fusion.5 = bf16[2,1,104,1152]{2,3,0,1:T(8,128)(2,1)S(1)} fusion(bf16[2,1,104,384]{2,3,0,1:T(8,128)(2,1)} %get-tuple-element.33, bf16[2,1,104,384]{2,3,0,1:T(8,128)(2,1)} %get-tuple-element.34, bf16[2,1,104,384]{2,3,0,1:T(8,128)(2,1)} %get-tuple-element.35), kind=kLoop, calls=%fused_computation.34 | loop fusion | flops 1437696 | bytes 958464 | tf_op jit(solution)/shard_map/concatenate | solution.py:108
  86.6 1.2 %pad_maximum_fusion.6 = bf16[2,1,104,1152]{2,3,0,1:T(8,128)(2,1)S(1)} fusion(bf16[2,1,104,384]{2,3,0,1:T(8,128)(2,1)} %get-tuple-element.30, bf16[2,1,104,384]{2,3,0,1:T(8,128)(2,1)} %get-tuple-element.31, bf16[2,1,104,384]{2,3,0,1:T(8,128)(2,1)} %get-tuple-element.32), kind=kLoop, calls=%fused_computation.35 | loop fusion | flops 1437696 | bytes 958464 | tf_op jit(solution)/shard_map/concatenate | solution.py:108
  87.8 1.1 copy.125
  88.9 1.2 %pad_maximum_fusion.7 = bf16[2,1,104,1152]{2,3,0,1:T(8,128)(2,1)S(1)} fusion(bf16[2,1,104,384]{2,3,0,1:T(8,128)(2,1)} %get-tuple-element.27, bf16[2,1,104,384]{2,3,0,1:T(8,128)(2,1)} %get-tuple-element.28, bf16[2,1,104,384]{2,3,0,1:T(8,128)(2,1)} %get-tuple-element.29), kind=kLoop, calls=%fused_computation.36 | loop fusion | flops 1437696 | bytes 958464 | tf_op jit(solution)/shard_map/concatenate | solution.py:108
  90.2 1.0 copy.127
  91.2 1.1 pad_maximum_fusion.8
  92.3 1.0 copy.129
  93.4 1.6 %fusion.39 = f32[208,192]{0,1:T(8,128)S(1)} fusion(bf16[208,1152]{1,0:T(8,128)(2,1)} %bitcast.162, bf16[1152,192]{0,1:T(8,128)(2,1)} %bitcast.163), kind=kOutput, calls=%fused_computation.102 | convolution fusion | flops 92012544 | bytes 1081344 | tf_op jit(solution)/shard_map/dot_general | solution.py:109
  99.9 4.9 %all-reduce.2 = (f32[2,16]{1,0:T(2,128)S(1)}, f32[2,16]{1,0:T(2,128)S(1)}) all-reduce(f32[2,16]{1,0:T(2,128)S(1)} %copy.133, f32[2,16]{1,0:T(2,128)S(1)} %copy.131), channel_id=1, replica_groups=mesh['video'=2,'block'=4,'band'=2,'chan'=2] {'band'}, use_global_device_ids=true, to_apply=%region_13.14 | all-reduce | flops 64 | bytes 512 | tf_op jit(solution)/shard_map/psum | solution.py:50
  105.4 14.3 %all_gather.11 = bf16[8,1,104,192]{2,3,1,0:T(8,128)(2,1)S(1)} all-gather(bf16[2,1,104,192]{2,3,1,0:T(8,128)(2,1)S(1)} %multiply_convert_fusion.1), channel_id=1, replica_groups=mesh['video'=2,'block'=4,'band'=2,'chan'=2] {'block'}, dimensions={0}, use_global_device_ids=true | all-gather | bytes 399360 | tf_op jit(solution)/shard_map/all_gather | solution.py:159
  120.4 0.8 fusion.17
  (131 shorter events, 18.7 us)
Async XLA Ops:
  0.0 29.9 %copy-start = (bf16[3,3,3,16,384]{4,3,2,1,0:T(8,128)(2,1)S(1)}, bf16[3,3,3,16,384]{4,3,2,1,0:T(8,128)(2,1)}, u32[]{:S(2)}) copy-start(bf16[3,3,3,16,384]{4,3,2,1,0:T(8,128)(2,1)} %param.10) | copy-start | bytes 995332
  19.5 15.0 %collective-permute-start.1 = (bf16[6,1,1664]{2,0,1:T(8,128)(2,1)S(1)}, bf16[6,1,1664]{2,0,1:T(8,128)(2,1)S(1)}, u32[]{:S(2)}, u32[]{:S(2)}) collective-permute-start(bf16[6,1,1664]{2,0,1:T(8,128)(2,1)S(1)} %fusion.21), channel_id=1, source_target_pairs={{2,0},{3,1},{6,4},{7,5},{10,8},{11,9},{14,12},{15,13},{18,16},{19,... | collective-permute-start | bytes 59912 | tf_op jit(solution)/shard_map/ppermute | solution.py:24
  20.8 13.9 %collective-permute-start = (bf16[6,1,1664]{2,0,1:T(8,128)(2,1)S(1)}, bf16[6,1,1664]{2,0,1:T(8,128)(2,1)S(1)}, u32[]{:S(2)}, u32[]{:S(2)}) collective-permute-start(bf16[6,1,1664]{2,0,1:T(8,128)(2,1)S(1)} %fusion.21), channel_id=1, source_target_pairs={{0,2},{1,3},{4,6},{5,7},{8,10},{9,11},{12,14},{13,15},{16,18},{17,... | collective-permute-start | bytes 59912 | tf_op jit(solution)/shard_map/ppermute | solution.py:22
  26.4 6.8 %copy-start.25 = (f32[384]{0:T(512)S(1)}, f32[384]{0:T(512)}, u32[]{:S(2)}) copy-start(f32[384]{0:T(512)} %param.12) | copy-start | bytes 4612
  26.4 7.5 %copy-start.26 = (f32[384]{0:T(512)S(1)}, f32[384]{0:T(512)}, u32[]{:S(2)}) copy-start(f32[384]{0:T(512)} %param.11) | copy-start | bytes 4612
  35.1 7.5 %copy-start.16 = (bf16[4,1,104,16]{3,2,0,1:T(8,128)(2,1)S(1)}, bf16[4,1,104,16]{3,2,0,1:T(8,128)(2,1)}, u32[]{:S(2)}) copy-start(bf16[4,1,104,16]{3,2,0,1:T(8,128)(2,1)} %get-tuple-element.69) | copy-start | bytes 39940
  35.1 7.5 %copy-start.17 = (bf16[4,1,104,16]{3,2,0,1:T(8,128)(2,1)S(1)}, bf16[4,1,104,16]{3,2,0,1:T(8,128)(2,1)}, u32[]{:S(2)}) copy-start(bf16[4,1,104,16]{3,2,0,1:T(8,128)(2,1)} %get-tuple-element.70) | copy-start | bytes 39940
  35.1 7.5 %copy-start.18 = (bf16[4,1,104,16]{3,2,0,1:T(8,128)(2,1)S(1)}, bf16[4,1,104,16]{3,2,0,1:T(8,128)(2,1)}, u32[]{:S(2)}) copy-start(bf16[4,1,104,16]{3,2,0,1:T(8,128)(2,1)} %get-tuple-element.71) | copy-start | bytes 39940
  46.5 7.9 %copy-start.19 = (f32[192]{0:T(256)S(1)}, f32[192]{0:T(256)}, u32[]{:S(2)}) copy-start(f32[192]{0:T(256)} %dynamic_slice.11) | copy-start | bytes 2308
  46.5 7.9 %copy-start.20 = (f32[192]{0:T(256)S(1)}, f32[192]{0:T(256)}, u32[]{:S(2)}) copy-start(f32[192]{0:T(256)} %dynamic_slice.10) | copy-start | bytes 2308
  46.5 7.9 %copy-start.27 = (pred[4]{0:T(512)(128)(4,1)S(1)}, pred[4]{0:T(512)(128)(4,1)}, u32[]{:S(2)}) copy-start(pred[4]{0:T(512)(128)(4,1)} %add_compare_fusion) | copy-start | bytes 16
  46.5 15.8 %copy-start.14 = (bf16[1,1,3,384,192]{3,4,2,1,0:T(8,128)(2,1)S(1)}, bf16[1,1,3,384,192]{3,4,2,1,0:T(8,128)(2,1)}, u32[]{:S(2)}) copy-start(bf16[1,1,3,384,192]{3,4,2,1,0:T(8,128)(2,1)} %get-tuple-element.22) | copy-start | bytes 1327108
  55.8 18.1 %collective-permute-start.3 = (bf16[4,1,104,192]{2,3,0,1:T(8,128)(2,1)S(1)}, bf16[4,1,104,192]{2,3,0,1:T(8,128)(2,1)S(1)}, u32[]{:S(2)}, u32[]{:S(2)}) collective-permute-start(bf16[4,1,104,192]{2,3,0,1:T(8,128)(2,1)S(1)} %select_bitcast_fusion), channel_id=1, source_target_pairs={{2,0},{3,1},{6,4},{7,5},{10,8},{11,9},{14,12},{15,13},{18,16},{19,... | collective-permute-start | bytes 479240 | tf_op jit(solution)/shard_map/ppermute | solution.py:24
  57.1 16.8 %collective-permute-start.2 = (bf16[4,1,104,192]{2,3,0,1:T(8,128)(2,1)S(1)}, bf16[4,1,104,192]{2,3,0,1:T(8,128)(2,1)S(1)}, u32[]{:S(2)}, u32[]{:S(2)}) collective-permute-start(bf16[4,1,104,192]{2,3,0,1:T(8,128)(2,1)S(1)} %select_bitcast_fusion), channel_id=1, source_target_pairs={{0,2},{1,3},{4,6},{5,7},{8,10},{9,11},{12,14},{13,15},{16,18},{17,... | collective-permute-start | bytes 479240 | tf_op jit(solution)/shard_map/ppermute | solution.py:22
  62.7 1.1 copy-start.13
  64.2 1.1 copy-start.12
  80.9 0.9 copy-start.15
  93.4 1.6 %copy-start.4 = (bf16[24,8,3,384]{3,1,2,0:T(8,128)(2,1)S(1)}, bf16[24,8,3,384]{3,1,2,0:T(8,128)(2,1)}, u32[]{:S(2)}) copy-start(bf16[24,8,3,384]{3,1,2,0:T(8,128)(2,1)} %copy.139) | copy-start | bytes 1327108
  93.4 1.9 %copy-start.5 = (bf16[24,8,3,384]{3,1,2,0:T(8,128)(2,1)S(1)}, bf16[24,8,3,384]{3,1,2,0:T(8,128)(2,1)}, u32[]{:S(2)}) copy-start(bf16[24,8,3,384]{3,1,2,0:T(8,128)(2,1)} %copy.140) | copy-start | bytes 1327108
  94.9 1.0 copy-start.6
  95.3 1.0 copy-start.7
  96.0 1.0 copy-start.8
  96.3 1.1 copy-start.1
  96.4 1.2 copy-start.9
  97.0 1.1 copy-start.2
  97.0 1.2 %copy-start.10 = (bf16[24,8,3,384]{3,1,2,0:T(8,128)(2,1)S(1)}, bf16[24,8,3,384]{3,1,2,0:T(8,128)(2,1)}, u32[]{:S(2)}) copy-start(bf16[24,8,3,384]{3,1,2,0:T(8,128)(2,1)} %copy.145) | copy-start | bytes 1327108
  97.5 1.1 copy-start.3
  97.5 1.2 %copy-start.11 = (bf16[24,8,3,384]{3,1,2,0:T(8,128)(2,1)S(1)}, bf16[24,8,3,384]{3,1,2,0:T(8,128)(2,1)}, u32[]{:S(2)}) copy-start(bf16[24,8,3,384]{3,1,2,0:T(8,128)(2,1)} %copy.146) | copy-start | bytes 1327108
  98.8 6.4 %copy-start.23 = (f32[192]{0:T(256)S(1)}, f32[192]{0:T(256)}, u32[]{:S(2)}) copy-start(f32[192]{0:T(256)} %param.15) | copy-start | bytes 2308
  98.8 6.4 %copy-start.24 = (f32[192]{0:T(256)S(1)}, f32[192]{0:T(256)}, u32[]{:S(2)}) copy-start(f32[192]{0:T(256)} %param.14) | copy-start | bytes 2308
  99.1 21.3 %copy-start.21 = (pred[4]{0:T(512)(128)(4,1)S(1)}, pred[4]{0:T(512)(128)(4,1)}, u32[]{:S(2)}) copy-start(pred[4]{0:T(512)(128)(4,1)} %get-tuple-element.84) | copy-start | bytes 16
  99.1 21.3 %copy-start.22 = (pred[4]{0:T(512)(128)(4,1)S(1)}, pred[4]{0:T(512)(128)(4,1)}, u32[]{:S(2)}) copy-start(pred[4]{0:T(512)(128)(4,1)} %get-tuple-element.85) | copy-start | bytes 16
where the time goes:
time: 122 us; the launch traced here: 121 us
  local copies, waits for them, and re-layouts  44.2 us (36%)
  blocking collectives  42.1 us (35%)
  other arithmetic  16.3 us (13%)
  starting transfers between devices  11.7 us (10%)
  matrix products  6.32 us (5%)
    all_gather x1, blocking collectives, shards(): all_slots = lax.all_gather(latents, 'block', axis=0, tiled=True)  15.1 us
    all_gather x1, blocking collectives, shards(): piece = lax.all_gather(even_norm, 'block', axis=0, tiled=True)  14.3 us
    unnamed x67, local copies, waits for them, and re-layouts  11 us
    psum x2, blocking collectives, group_silu(): lax.psum((jnp.sum(grouped, axis=(1, 3)), jnp.sum(grouped * grouped, axis=...  9.83 us
    ppermute x2, starting transfers between devices, with_halo(): lax.ppermute(tail, axis, [(i, (i + 1) % count) for i in range(ends)])  9.11 us
    slice x10, local copies, waits for them, and re-layouts, latent_conv(): latent_grid[step_t:step_t + out_frames, step_y:step_y + band_rows, step_x...  8.19 us
    concatenate x9, other arithmetic, weighted_taps(): stacked = jnp.concatenate(patches, axis=-1).reshape(-1, 3 * in_width)  7.39 us
    slice x10, local copies, waits for them, and re-layouts, weighted_taps(): kernel[step_t, step_y].reshape(3 * in_width, out_width)  6.99 us
  transfers between devices with their start and end apart: 4, of which 0 were waited for; matrix products, arithmetic and copies ran while one was open for 17% of the time, Pallas kernels for 0%

commit v1 on v0

v1 whole, which is shorter than its diff:
```python
import functools

import jax
import jax.numpy as jnp
from jax import lax
from jax.experimental import pallas as pl
from jax.experimental.pallas import tpu as pltpu
from jax.sharding import PartitionSpec as P

LAT = 16
C = 384
GROUPS = 32
WIDTH = C // GROUPS
EPSILON = 1e-06
LANES = 128
COLS_IN_TILE = LANES // LAT


def ring_place(chip_block, chip_band, blocks):
    return jnp.where(chip_band == 0, chip_block, 2 * blocks - 1 - chip_block)


def ring_moves(blocks, shift_first, shift_second):
    ring = [(b, 0) for b in range(blocks)] + [(b, 1) for b in reversed(range(blocks))]
    count = len(ring)
    moves = []
    for core, shift in ((0, shift_first), (1, shift_second)):
        for place in range(count):
            b, a = ring[place]
            b2, a2 = ring[(place + shift) % count]
            moves.append(((b * 2 + a) * 2 + core, (b2 * 2 + a2) * 2 + core))
    return moves


def pack_body(*refs):
    out = refs[-1]
    for i, ref in enumerate(refs[:-1]):
        out[i] = ref[0]


def pack(*parts):
    vmem = pl.BlockSpec(memory_space=pltpu.VMEM)
    return pl.pallas_call(
        pack_body,
        out_shape=jax.ShapeDtypeStruct((len(parts),) + parts[0].shape[1:], parts[0].dtype),
        in_specs=[vmem] * len(parts),
        out_specs=vmem,
        compiler_params=pltpu.CompilerParams(vmem_limit_bytes=1024 * 1024),
    )(*parts)


def exchange_ring(latents, kept):
    axes = ("block", "band", "chan")
    blocks = lax.axis_size("block")
    swap = [(2 * n + c, 2 * n + 1 - c) for n in range(2 * blocks) for c in range(2)]
    own = latents
    first = lax.ppermute(own, axes, ring_moves(blocks, 1, 2))
    second = lax.ppermute(first, axes, swap)
    held = pack(kept, first, second)
    third = lax.ppermute(held, axes, ring_moves(blocks, 3, 6))
    fourth = lax.ppermute(third, axes, swap)
    return [kept, first, second, third, fourth]


def piece_ring(block, band, owner, row, blocks):
    core = lax.axis_index("chan")
    count = 2 * blocks
    mine = ring_place(block, band, blocks)
    other = ring_place(owner, row, blocks)
    back = lax.rem(mine - other + count, count)
    base = jnp.where(back >= 6, 2, jnp.where(back >= 3, 1, 0))
    rest = back - 3 * base
    group = jnp.where(base == 0, 0, jnp.where(core == 0, base, 3 - base))
    order = jnp.where(base == 0, core, base - 1)
    place = jnp.where((order == 0) | (rest == 0), rest, 3 - rest)
    return group * 3 + place


def group_matrix(width):
    rows = lax.broadcasted_iota(jnp.int32, (width, width), 0)
    cols = lax.broadcasted_iota(jnp.int32, (width, width), 1)
    low = cols - lax.rem(cols, WIDTH)
    same = (rows >= low) & (rows < low + WIDTH)
    return jnp.where(same, 1.0, 0.0).astype(jnp.bfloat16)


def group_sums(sums, matrix):
    high = sums.astype(jnp.bfloat16)
    rest = sums - high.astype(jnp.float32)
    middle = rest.astype(jnp.bfloat16)
    low = (rest - middle.astype(jnp.float32)).astype(jnp.bfloat16)
    rows = sums.shape[0]
    parts = jnp.concatenate([high, middle, low], axis=0)
    out = jnp.dot(parts, matrix, preferred_element_type=jnp.float32)
    return out[:rows] + out[rows : 2 * rows] + out[2 * rows :]


def silu(u):
    return u / (1.0 + jnp.exp(-u))


def prepare_body(rows, *refs):
    latents, w_in, gain_in, shift_in, w_mid, gain_out, shift_out = refs[:7]
    own, wide, matrix, kernel, flat_terms, tall_terms = refs[7:13]
    small, flat_parts, tall_parts, sems = refs[13:]
    half = tall_terms.shape[1]
    depth = wide.shape[0] // 3
    pairs = (
        (latents, own),
        (w_in, small),
        (gain_in, flat_parts.at[0]),
        (shift_in, flat_parts.at[1]),
        (gain_out, tall_parts.at[0]),
        (shift_out, tall_parts.at[1]),
        (w_mid, kernel),
    )
    loads = [pltpu.make_async_copy(a, b, sems.at[i]) for i, (a, b) in enumerate(pairs)]
    for load in loads:
        load.start()
    wide[...] = jnp.zeros_like(wide)
    matrix[...] = group_matrix(C)
    eye = lax.broadcasted_iota(jnp.int32, (half, half), 0) == lax.broadcasted_iota(
        jnp.int32, (half, half), 1
    )
    for load in loads[:-1]:
        load.wait()
    for t in range(3):
        for place in range(rows):
            for r in range(rows):
                y = place - r + 1
                if 0 <= y <= 2:
                    top = t * depth + place * 64
                    wide[top : top + 3 * LAT, r * C : (r + 1) * C] = small[t, y]
    for i in range(2):
        flat_terms[i : i + 1] = flat_parts[i].reshape(1, C)
        spread = jnp.where(eye, tall_parts[i].reshape(1, half), 0.0)
        tall_terms[i] = jnp.broadcast_to(jnp.sum(spread, axis=1, keepdims=True), (half, LANES))
    loads[-1].wait()


def prepare(rows, own, w_in, gain_in, shift_in, w_mid, gain_out, shift_out):
    half = w_mid.shape[4]
    pairs = -(-rows // 2)
    small = (3, 3, 3 * LAT, C)
    operands = (
        own,
        w_in.reshape(small),
        gain_in,
        shift_in,
        jnp.transpose(w_mid, (0, 1, 2, 4, 3)).reshape(3, 3, 3 * half, C),
        gain_out,
        shift_out,
    )
    return pl.pallas_call(
        functools.partial(prepare_body, rows),
        out_shape=(
            pltpu.VMEM(own.shape, own.dtype),
            pltpu.VMEM((3 * pairs * LANES, rows * C), jnp.bfloat16),
            pltpu.VMEM((C, C), jnp.bfloat16),
            pltpu.VMEM((3, 3, 3 * half, C), jnp.bfloat16),
            pltpu.VMEM((8, C), jnp.float32),
            pltpu.VMEM((2, half, LANES), jnp.float32),
        ),
        in_specs=[pl.BlockSpec(memory_space=pltpu.HBM)] * 7,
        out_specs=(pl.BlockSpec(memory_space=pltpu.VMEM),) * 6,
        scratch_shapes=[
            pltpu.VMEM(small, jnp.bfloat16),
            pltpu.VMEM((2, C), jnp.float32),
            pltpu.VMEM((2, half), jnp.float32),
            pltpu.SemaphoreType.DMA((7,)),
        ],
        compiler_params=pltpu.CompilerParams(vmem_limit_bytes=16 * 1024 * 1024),
    )(*[pltpu.with_memory_space_constraint(a, pltpu.HBM) for a in operands])


def body(cfg, *refs):
    blocks, rows, frames, columns, pieces, use_ring = cfg
    n_arrays = len(pieces)
    sources = refs[:n_arrays]
    (counts_in, wide, matrix, kernel, flat_terms, tall_terms, out) = refs[n_arrays : n_arrays + 7]
    (counts, slabs, patches, first, acts, second, sem) = refs[n_arrays + 7 :]
    half = out.shape[2]
    chunks = columns // COLS_IN_TILE
    slab = -(-(chunks + 1) // 8) * 8
    padded = -(-(columns + 1) // 16) * 16
    stride = -(-(columns + 1) // LANES) * LANES
    halo = 4
    lat_frames = frames + halo
    act_frames = frames + 2
    pairs = -(-rows // 2)
    depth = pairs * LANES
    own_rows = out.shape[1]
    block = lax.axis_index("block")
    band = lax.axis_index("band")

    load = pltpu.make_async_copy(counts_in, counts, sem)
    load.start()

    slabs[...] = jnp.zeros_like(slabs)
    at = 0
    for source, n in zip(sources, pieces):
        for p in range(n):
            values = source[p].astype(jnp.float32)
            for b in range(chunks):
                slabs[pl.ds(at * frames * slab + b, frames, stride=slab), :] = values[
                    :, b * LANES : (b + 1) * LANES
                ]
            at += 1

    load.wait()
    my_start = jnp.int32(0)
    for k in range(blocks):
        my_start = my_start + jnp.where(k < block, counts[k], 0)
    my_count = counts[block]

    lane = lax.broadcasted_iota(jnp.int32, (slab, LANES), 1)
    patches[...] = jnp.zeros_like(patches)
    for f in range(lat_frames):
        if f < halo:
            wanted = my_start - halo + f
            valid = wanted >= 0
            safe = jnp.maximum(wanted, 0)
            total, begin, owner = jnp.int32(0), jnp.int32(0), jnp.int32(0)
            for k in range(blocks):
                total = total + counts[k]
                past = safe >= total
                owner = owner + jnp.where(past, 1, 0)
                begin = jnp.where(past, total, begin)
            slot = safe - begin
        else:
            valid, owner, slot = None, block, jnp.int32(f - halo)
        planes = []
        for r in range(rows):
            rank, inner = r // own_rows, r % own_rows
            if use_ring:
                piece = piece_ring(block, band, owner, rank, blocks)
            else:
                piece = owner * (rows // own_rows) + rank
            piece = piece * own_rows + inner
            top = pl.multiple_of((piece * frames + slot) * slab, 8)
            plane = slabs[pl.ds(top, slab), :]
            if valid is not None:
                plane = jnp.where(valid, plane, 0.0)
            planes.append(plane)
        if rows % 2:
            planes.append(jnp.zeros_like(planes[0]))
        for g in range(pairs):
            left, right = planes[2 * g], pltpu.roll(planes[2 * g + 1], 64, 1)
            for j in range(COLS_IN_TILE):
                begin_lane = LAT * (j - 1)
                a, b = left, right
                if j == 0:
                    a = jnp.where(lane >= LANES - LAT, pltpu.roll(left, 1, 0), left)
                    b = jnp.where(
                        (lane >= 64 - LAT) & (lane < 64), pltpu.roll(right, 1, 0), right
                    )
                if j == COLS_IN_TILE - 1:
                    a = jnp.where(lane < LAT, pltpu.roll(left, slab - 1, 0), left)
                    b = jnp.where(
                        (lane >= 64) & (lane < 64 + LAT), pltpu.roll(right, slab - 1, 0), right
                    )
                low = begin_lane % LANES
                if low + 64 <= LANES:
                    inside = (lane >= low) & (lane < low + 64)
                else:
                    inside = (lane >= low) | (lane < low + 64 - LANES)
                mixed = pltpu.roll(jnp.where(inside, a, b), (-begin_lane) % LANES, 1)
                patches[
                    pl.ds((g * lat_frames + f) * padded + j, chunks, stride=COLS_IN_TILE), :
                ] = mixed[:chunks]

    low_patches = patches[...].astype(jnp.bfloat16)
    stacked = jnp.concatenate(
        [
            low_patches[(g * lat_frames + t) * padded : (g * lat_frames + t + act_frames) * padded]
            for t in range(3)
            for g in range(pairs)
        ],
        axis=1,
    )
    first[...] = jnp.dot(stacked, wide[...], preferred_element_type=jnp.float32)

    sums, squares = [], []
    for g in range(act_frames):
        plain = jnp.zeros((1, C), jnp.float32)
        square = jnp.zeros((1, C), jnp.float32)
        for r in range(rows):
            part = first[g * padded : (g + 1) * padded, r * C : (r + 1) * C]
            plain = plain + jnp.sum(part, axis=0, keepdims=True)
            square = square + jnp.sum(part * part, axis=0, keepdims=True)
        sums.append(plain)
        squares.append(square)
    fill = [jnp.zeros((1, C), jnp.float32)] * (-(2 * act_frames) % 16)
    totals = group_sums(jnp.concatenate(sums + squares + fill, axis=0), matrix[...])
    size = float(rows * columns * WIDTH)
    mean = totals[:act_frames] / size
    variance = totals[act_frames : 2 * act_frames] / size - mean * mean
    scale = lax.rsqrt(variance + EPSILON) * flat_terms[0:1]
    shift = flat_terms[1:2] - mean * scale
    for g in range(act_frames):
        live = my_start - 2 + g >= 0
        scale_g = jnp.where(live, scale[g : g + 1], 0.0)
        shift_g = jnp.where(live, shift[g : g + 1], 0.0)
        for r in range(rows):
            part = first[g * padded : g * padded + columns, r * C : (r + 1) * C]
            act = silu(part * scale_g + shift_g)
            act = jnp.concatenate([act, jnp.zeros((stride - columns, C), jnp.float32)], axis=0)
            acts[g * stride : (g + 1) * stride, r * C : (r + 1) * C] = act.astype(jnp.bfloat16)

    span = frames * stride
    inside = lax.broadcasted_iota(jnp.int32, (half, stride), 1) < columns
    spans = {}
    for r in range(rows):
        spans.setdefault((max(0, r - 1), min(rows - 1, r + 1)), []).append(r)
    for (low, high), members in spans.items():
        places = range(low, high + 1)
        positions = jnp.concatenate(
            [
                acts[t * stride : t * stride + span, place * C : (place + 1) * C]
                for place in places
                for t in range(3)
            ],
            axis=1,
        )
        weights = jnp.concatenate(
            [
                jnp.concatenate(
                    [kernel[t, place - r + 1] for place in places for t in range(3)], axis=1
                )
                for r in members
            ],
            axis=0,
        )
        taps = lax.dot_general(
            weights, positions, (((1,), (1,)), ((), ())), preferred_element_type=jnp.float32
        )
        for m, r in enumerate(members):
            top = m * 3 * half
            for f in range(frames):
                left = f * stride
                tap = [
                    taps[top + s * half : top + (s + 1) * half, left : left + stride]
                    for s in range(3)
                ]
                value = tap[1] + pltpu.roll(tap[0], 1, 1) + pltpu.roll(tap[2], stride - 1, 1)
                second[r, f] = jnp.where(inside, value, 0.0)

    lane_at = lax.broadcasted_iota(jnp.int32, (half, LANES), 1)
    columns_of = jnp.zeros((half, LANES), jnp.float32)
    for f in range(frames):
        plain, square = second[0, f], second[0, f] * second[0, f]
        for r in range(1, rows):
            plain = plain + second[r, f]
            square = square + second[r, f] * second[r, f]
        columns_of = jnp.where(lane_at == f, jnp.sum(plain, axis=1, keepdims=True), columns_of)
        columns_of = jnp.where(
            lane_at == frames + f, jnp.sum(square, axis=1, keepdims=True), columns_of
        )
    high = columns_of.astype(jnp.bfloat16)
    rest = columns_of - high.astype(jnp.float32)
    middle = rest.astype(jnp.bfloat16)
    low = (rest - middle.astype(jnp.float32)).astype(jnp.bfloat16)
    matrix2 = matrix[:half, :half]
    totals = (
        jnp.dot(matrix2, high, preferred_element_type=jnp.float32)
        + jnp.dot(matrix2, middle, preferred_element_type=jnp.float32)
        + jnp.dot(matrix2, low, preferred_element_type=jnp.float32)
    )
    mean = totals / size
    variance = pltpu.roll(mean, LANES - frames, 1) - mean * mean
    scale = lax.rsqrt(variance + EPSILON) * tall_terms[0]
    shift = tall_terms[1] - mean * scale
    for f in range(frames):
        for inner in range(own_rows):
            part = second[band * own_rows + inner, f]
            value = silu(part * scale[:, f : f + 1] + shift[:, f : f + 1])
            value = jnp.where(f < my_count, value, 0.0).astype(out.dtype)
            out[f, inner] = value[:, :columns]


def shards(latents, frame_counts, w_in, gain_in, shift_in, w_mid, gain_out, shift_out):
    frames, own_rows, flat = latents.shape
    columns = flat // LAT
    half = w_mid.shape[4]
    blocks, bands = lax.axis_size("block"), lax.axis_size("band")
    rows = own_rows * bands
    use_ring = blocks == 4 and bands == 2 and own_rows == 1 and lax.axis_size("chan") == 2
    own = jnp.transpose(latents, (1, 0, 2))
    kept, *prepared = prepare(rows, own, w_in, gain_in, shift_in, w_mid, gain_out, shift_out)
    if use_ring:
        sources = exchange_ring(own, kept)
    else:
        gathered = lax.all_gather(own, ("block", "band"), axis=0)
        sources = [gathered.reshape(-1, frames, flat)]
    pieces = tuple(a.shape[0] for a in sources)
    chunks = columns // COLS_IN_TILE
    slab = -(-(chunks + 1) // 8) * 8
    padded = -(-(columns + 1) // 16) * 16
    stride = -(-(columns + 1) // LANES) * LANES
    pairs = -(-rows // 2)
    cfg = (blocks, rows, frames, columns, pieces, use_ring)
    vmem = pl.BlockSpec(memory_space=pltpu.VMEM)
    decoded = pl.pallas_call(
        functools.partial(body, cfg),
        out_shape=jax.ShapeDtypeStruct((frames, own_rows, half, columns), jnp.bfloat16),
        in_specs=[vmem] * len(sources)
        + [pl.BlockSpec(memory_space=pltpu.HBM)]
        + [vmem] * 5,
        out_specs=vmem,
        scratch_shapes=[
            pltpu.SMEM((blocks,), jnp.int32),
            pltpu.VMEM((sum(pieces) * frames * slab, LANES), jnp.float32),
            pltpu.VMEM((pairs * (frames + 4) * padded, LANES), jnp.float32),
            pltpu.VMEM(((frames + 2) * padded, rows * C), jnp.float32),
            pltpu.VMEM(((frames + 2) * stride, rows * C), jnp.bfloat16),
            pltpu.VMEM((rows, frames, half, stride), jnp.float32),
            pltpu.SemaphoreType.DMA,
        ],
        compiler_params=pltpu.CompilerParams(vmem_limit_bytes=32 * 1024 * 1024),
    )(*sources, pltpu.with_memory_space_constraint(frame_counts, pltpu.HBM), *prepared)
    return jnp.transpose(decoded, (0, 1, 3, 2))


def solution(mesh):
    return jax.shard_map(
        shards,
        mesh=mesh,
        in_specs=(
            P(("video", "block"), "band", None),
            P("video"),
            P(),
            P(),
            P(),
            P(None, None, None, None, "chan"),
            P("chan"),
            P("chan"),
        ),
        out_specs=P(("video", "block"), "band", None, "chan"),
        check_vma=False,
    )
```

time: 122 us -> 21.5 us (0.18)
  local copies, waits for them, and re-layouts: 44.2 us -> 0 us
  blocking collectives: 42.1 us -> 0 us
  other arithmetic: 16.3 us -> 0 us
  Pallas kernels: 0 us -> 9.11 us
  matrix products: 6.32 us -> 0 us
  waiting for transfers between devices: 0.01 us -> 4.84 us
  starting transfers between devices: 11.7 us -> 7.31 us
    all_gather x3 -> x0, blocking collectives: 32.3 us -> none  [the longest x1 15.1 us: shards(): all_slots = lax.all_gather(latents, 'block', axis=0, tiled=True)]
    slice x22 -> x0, local copies, waits for them, and re-layouts: 17.8 us -> none  [the longest x10 8.19 us: latent_conv(): latent_grid[step_t:step_t + out_frames, step_y:step_y + band_rows, step_x...]
    unnamed x67 -> x0, local copies, waits for them, and re-layouts: 11 us -> none
    concatenate x12 -> x0, local copies, waits for them, and re-layouts: 9.93 us -> none  [the longest x9 5.64 us: weighted_taps(): stacked = jnp.concatenate(patches, axis=-1).reshape(-1, 3 * in_width)]
    psum x2 -> x0, blocking collectives: 9.83 us -> none  [group_silu(): lax.psum((jnp.sum(grouped, axis=(1, 3)), jnp.sum(grouped * grouped, axis=...]
    pallas_call x0 -> x3, Pallas kernels: none -> 9.11 us  [the longest x1 6.72 us: shards(): pl.pallas_call(functools.partial(body, cfg), out_shape=jax.ShapeDtypeStru...]
    concatenate x11 -> x0, other arithmetic: 7.89 us -> none  [the longest x9 7.39 us: weighted_taps(): stacked = jnp.concatenate(patches, axis=-1).reshape(-1, 3 * in_width)]
    dot_general x10 -> x0, matrix products: 6.32 us -> none  [the longest x9 4.12 us: weighted_taps(): jnp.dot(stacked, kernel[step_t, step_y].reshape(3 * in_width, out_width),...]
  transfers between devices with their start and end apart: 4 -> 4, of which waited for: 0 -> 3; matrix products, arithmetic and copies ran while one was open for 17% -> 0% of each run, Pallas kernels for 0% -> 11%
where the time goes in v1:
time: 21.5 us; the launch traced here: 21.3 us
  Pallas kernels  9.11 us (42%)
  starting transfers between devices  7.31 us (34%)
  waiting for transfers between devices  4.84 us (23%)
    pallas_call x1, Pallas kernels, shards(): pl.pallas_call(functools.partial(body, cfg), out_shape=jax.ShapeDtypeStru...  6.72 us
    ppermute x1, starting transfers between devices, exchange_ring(): third = lax.ppermute(held, axes, ring_moves(blocks, 3, 6))  4.25 us
    ppermute x1, starting transfers between devices, exchange_ring(): first = lax.ppermute(own, axes, ring_moves(blocks, 1, 2))  3.05 us
    pallas_call x1, Pallas kernels, prepare(): pl.pallas_call(functools.partial(prepare_body, rows), out_shape=(pltpu.VM...  2.39 us
    ppermute x1, waiting for transfers between devices, exchange_ring(): third = lax.ppermute(held, axes, ring_moves(blocks, 3, 6))  1.82 us
    ppermute x1, waiting for transfers between devices, exchange_ring(): first = lax.ppermute(own, axes, ring_moves(blocks, 1, 2))  1.81 us
    ppermute x1, waiting for transfers between devices, exchange_ring(): fourth = lax.ppermute(third, axes, swap)  1.21 us
  transfers between devices with their start and end apart: 4, of which 3 were waited for; matrix products, arithmetic and copies ran while one was open for 0% of the time, Pallas kernels for 11%

profile of v1, /device:TPU:0, one launch (start us, length us, event | category | flops | bytes accessed | tf_op | source)
XLA Modules:
  0.0 21.3 jit_solution(15955686811197382685)
XLA Ops:
  0.0 3.1 %collective-permute-start = (bf16[1,4,1664]{2,1,0:T(4,128)(2,1)}, bf16[1,4,1664]{2,1,0:T(4,128)(2,1)S(1)}, u32[]{:S(2)}, u32[]{:S(2)}) collective-permute-start(bf16[1,4,1664]{2,1,0:T(4,128)(2,1)} %bitcast.8), channel_id=1, source_target_pairs={{0,4},{4,8},{8,12},{12,14},{14,10},{10,6},{6,2},{2,0},{1,9},{5,13}... | collective-permute-start | bytes 39944 | tf_op jit(solution)/shard_map/ppermute | solution.py:57
  3.1 1.8 %collective-permute-done.refs_1_ = bf16[1,4,1664]{2,1,0:T(4,128)(2,1)S(1)} collective-permute-done((bf16[1,4,1664]{2,1,0:T(4,128)(2,1)}, bf16[1,4,1664]{2,1,0:T(4,128)(2,1)S(1)}, u32[]{:S(2)}, u32[]{:S(2)}) %collective-permute-start) | collective-permute-done | bytes 13344 | tf_op jit(solution)/shard_map/ppermute | solution.py:57
  4.9 0.0 collective-permute-start.1
  4.9 2.4 %shard_map.82 = (bf16[1,4,1664]{2,1,0:T(4,128)(2,1)S(1)}, bf16[384,768]{1,0:T(8,128)(2,1)S(1)}, bf16[384,384]{1,0:T(8,128)(2,1)S(1)}, bf16[3,3,576,384]{3,2,1,0:...) custom-call(bf16[1,4,1664]{2,1,0:T(4,128)(2,1)} %bitcast.9, bf16[3,3,48,384]{3,2,1,0:T(8,128)(2,1)} %bitcast.7, ...), custom_call_target="tpu_custom_call" | custom-call | tf_op jit(solution)/shard_map/pallas_call | solution.py:154
  7.3 0.0 collective-permute-done.1.refs_2_
  7.3 4.3 %collective-permute-start.2 = (bf16[3,4,1664]{2,1,0:T(4,128)(2,1)S(1)}, bf16[3,4,1664]{2,1,0:T(4,128)(2,1)S(1)}, u32[]{:S(2)}, u32[]{:S(2)}) collective-permute-start(bf16[3,4,1664]{2,1,0:T(4,128)(2,1)S(1)} %shard_map.83), channel_id=1, source_target_pairs={{0,12},{4,14},{8,10},{12,6},{14,2},{10,0},{6,4},{2,8},{1,7},{5,3},... | collective-permute-start | bytes 119816 | tf_op jit(solution)/shard_map/ppermute | solution.py:60
  11.5 1.8 %collective-permute-done.2.refs_3_ = bf16[3,4,1664]{2,1,0:T(4,128)(2,1)S(1)} collective-permute-done((bf16[3,4,1664]{2,1,0:T(4,128)(2,1)S(1)}, bf16[3,4,1664]{2,1,0:T(4,128)(2,1)S(1)}, u32[]{:S(2)}, u32[]{:S(2)}) %collective-permute-start.2) | collective-permute-done | bytes 39968 | tf_op jit(solution)/shard_map/ppermute | solution.py:60
  13.4 0.0 collective-permute-start.3
  13.4 1.2 %collective-permute-done.3.refs_4_ = bf16[3,4,1664]{2,1,0:T(4,128)(2,1)S(1)} collective-permute-done((bf16[3,4,1664]{2,1,0:T(4,128)(2,1)S(1)}, bf16[3,4,1664]{2,1,0:T(4,128)(2,1)S(1)}, u32[]{:S(2)}, u32[]{:S(2)}) %collective-permute-start.3) | collective-permute-done | bytes 39968 | tf_op jit(solution)/shard_map/ppermute | solution.py:61
  14.6 6.7 %shard_map.84 = bf16[4,1,192,104]{3,2,1,0:T(8,128)(2,1)} custom-call(bf16[1,4,1664]{2,1,0:T(4,128)(2,1)S(1)} %get-tuple-element.11.refs_0_, bf16[1,4,1664]{2,1,0:T(4,128)(2,1)S(1)} %collective-permute-done.refs_1_, bf16[1,4,1664]{2,1,0:T(4,128)(2,1)S(1)} %collective-permute-done.1.refs_2_, bf16[3,4,1664]{2,1,0:T(4,128)(2,1)S(1)} %collective-permute-done.2.refs_3_, ...), custom_call_target="tpu_custom_call" | custom-call | tf_op jit(solution)/shard_map/pallas_call | solution.py:403
  (1 shorter events, 0.0 us)
Async XLA Ops:
  0.0 4.9 %collective-permute-start = (bf16[1,4,1664]{2,1,0:T(4,128)(2,1)}, bf16[1,4,1664]{2,1,0:T(4,128)(2,1)S(1)}, u32[]{:S(2)}, u32[]{:S(2)}) collective-permute-start(bf16[1,4,1664]{2,1,0:T(4,128)(2,1)} %bitcast.8), channel_id=1, source_target_pairs={{0,4},{4,8},{8,12},{12,14},{14,10},{10,6},{6,2},{2,0},{1,9},{5,13}... | collective-permute-start | bytes 39944 | tf_op jit(solution)/shard_map/ppermute | solution.py:57
  4.9 2.4 %collective-permute-start.1 = (bf16[1,4,1664]{2,1,0:T(4,128)(2,1)S(1)}, bf16[1,4,1664]{2,1,0:T(4,128)(2,1)S(1)}, u32[]{:S(2)}, u32[]{:S(2)}) collective-permute-start(bf16[1,4,1664]{2,1,0:T(4,128)(2,1)S(1)} %collective-permute-done.refs_1_), channel_id=1, source_target_pairs={{0,1},{1,0},{2,3},{3,2},{4,5},{5,4},{6,7},{7,6},{8,9},{9,8},{10,11... | collective-permute-start | bytes 39944 | tf_op jit(solution)/shard_map/ppermute | solution.py:58
  7.3 6.1 %collective-permute-start.2 = (bf16[3,4,1664]{2,1,0:T(4,128)(2,1)S(1)}, bf16[3,4,1664]{2,1,0:T(4,128)(2,1)S(1)}, u32[]{:S(2)}, u32[]{:S(2)}) collective-permute-start(bf16[3,4,1664]{2,1,0:T(4,128)(2,1)S(1)} %shard_map.83), channel_id=1, source_target_pairs={{0,12},{4,14},{8,10},{12,6},{14,2},{10,0},{6,4},{2,8},{1,7},{5,3},... | collective-permute-start | bytes 119816 | tf_op jit(solution)/shard_map/ppermute | solution.py:60
  13.4 1.2 %collective-permute-start.3 = (bf16[3,4,1664]{2,1,0:T(4,128)(2,1)S(1)}, bf16[3,4,1664]{2,1,0:T(4,128)(2,1)S(1)}, u32[]{:S(2)}, u32[]{:S(2)}) collective-permute-start(bf16[3,4,1664]{2,1,0:T(4,128)(2,1)S(1)} %collective-permute-done.2.refs_3_), channel_id=1, source_target_pairs={{0,1},{1,0},{2,3},{3,2},{4,5},{5,4},{6,7},{7,6},{8,9},{9,8},{10,11... | collective-permute-start | bytes 119816 | tf_op jit(solution)/shard_map/ppermute | solution.py:61

commit v2 on v1

--- a/solution.py
+++ b/solution.py
@@ -6,6 +6,7 @@
 from jax.experimental import pallas as pl
 from jax.experimental.pallas import tpu as pltpu
 from jax.sharding import PartitionSpec as P
+
 
 LAT = 16
 C = 384
@@ -16,20 +17,61 @@
 COLS_IN_TILE = LANES // LAT
 
 
-def ring_place(chip_block, chip_band, blocks):
-    return jnp.where(chip_band == 0, chip_block, 2 * blocks - 1 - chip_block)
-
-
-def ring_moves(blocks, shift_first, shift_second):
-    ring = [(b, 0) for b in range(blocks)] + [(b, 1) for b in reversed(range(blocks))]
-    count = len(ring)
+FIRST_ROUND = (
+    ((0, 1), (2, 0), (1, 0), (3, 1)),
+    ((1, 1), (3, 0), (0, 0), (2, 0)),
+)
+SECOND_ROUND = (
+    ((1, 0), (0, 0), (3, 1), (2, 0)),
+    ((1, 0), (3, 0), (0, 0), (2, 1)),
+)
+
+
+def round_moves(sources):
     moves = []
-    for core, shift in ((0, shift_first), (1, shift_second)):
-        for place in range(count):
-            b, a = ring[place]
-            b2, a2 = ring[(place + shift) % count]
-            moves.append(((b * 2 + a) * 2 + core, (b2 * 2 + a2) * 2 + core))
+    for core in range(2):
+        for block in range(4):
+            for band in range(2):
+                from_block, turn = sources[core][block]
+                source = (from_block * 2 + (band ^ turn)) * 2 + core
+                moves.append((source, (block * 2 + band) * 2 + core))
     return moves
+
+
+def held_pieces(core, block):
+    return [(block, 0), FIRST_ROUND[core][block], FIRST_ROUND[1 - core][block]]
+
+
+def all_pieces(core, block):
+    pieces = held_pieces(core, block)
+    for who in (core, 1 - core):
+        from_block, turn = SECOND_ROUND[who][block]
+        pieces += [(b, t ^ turn) for b, t in held_pieces(who, from_block)]
+    return pieces
+
+
+def choose(index, values):
+    out = jnp.int32(values[0])
+    for i, value in enumerate(values[1:], 1):
+        out = jnp.where(index == i, value, out)
+    return out
+
+
+def piece_finder(bands, use_ring):
+    block, band = lax.axis_index("block"), lax.axis_index("band")
+    if not use_ring:
+        return lambda owner, rank: owner * bands + rank
+    mine = lax.axis_index("chan") * 4 + block
+    places = []
+    for owner in range(4):
+        for turn in range(2):
+            column = []
+            for core in range(2):
+                for at in range(4):
+                    found = all_pieces(core, at)
+                    column.append(found.index((owner, turn)) if (owner, turn) in found else 0)
+            places.append(choose(mine, column))
+    return lambda owner, rank: choose(owner * 2 + lax.rem(rank + band, 2), places)
 
 
 def pack_body(*refs):
@@ -51,29 +93,13 @@
 
 def exchange_ring(latents, kept):
     axes = ("block", "band", "chan")
-    blocks = lax.axis_size("block")
-    swap = [(2 * n + c, 2 * n + 1 - c) for n in range(2 * blocks) for c in range(2)]
-    own = latents
-    first = lax.ppermute(own, axes, ring_moves(blocks, 1, 2))
+    swap = [(2 * n + c, 2 * n + 1 - c) for n in range(8) for c in range(2)]
+    first = lax.ppermute(latents, axes, round_moves(FIRST_ROUND))
     second = lax.ppermute(first, axes, swap)
     held = pack(kept, first, second)
-    third = lax.ppermute(held, axes, ring_moves(blocks, 3, 6))
+    third = lax.ppermute(held, axes, round_moves(SECOND_ROUND))
     fourth = lax.ppermute(third, axes, swap)
     return [kept, first, second, third, fourth]
-
-
-def piece_ring(block, band, owner, row, blocks):
-    core = lax.axis_index("chan")
-    count = 2 * blocks
-    mine = ring_place(block, band, blocks)
-    other = ring_place(owner, row, blocks)
-    back = lax.rem(mine - other + count, count)
-    base = jnp.where(back >= 6, 2, jnp.where(back >= 3, 1, 0))
-    rest = back - 3 * base
-    group = jnp.where(base == 0, 0, jnp.where(core == 0, base, 3 - base))
-    order = jnp.where(base == 0, core, base - 1)
-    place = jnp.where((order == 0) | (rest == 0), rest, 3 - rest)
-    return group * 3 + place
 
 
 def group_matrix(width):
@@ -96,25 +122,31 @@
 
 
 def silu(u):
-    return u / (1.0 + jnp.exp(-u))
-
-
-def prepare_body(rows, *refs):
-    latents, w_in, gain_in, shift_in, w_mid, gain_out, shift_out = refs[:7]
-    own, wide, matrix, kernel, flat_terms, tall_terms = refs[7:13]
-    small, flat_parts, tall_parts, sems = refs[13:]
+    half_u = 0.5 * u
+    return half_u + half_u * jnp.tanh(half_u)
+
+
+HALO = 4
+
+
+def prepare_body(cfg, *refs):
+    blocks, rows, own_rows, frames, use_ring = cfg
+    latents, w_in, gain_in, shift_in, gain_out, shift_out, counts_in, w_mid = refs[:8]
+    own, wide, matrix, flat_terms, tall_terms, table, kernel = refs[8:15]
+    small, flat_parts, tall_parts, counts, sems = refs[15:]
     half = tall_terms.shape[1]
     depth = wide.shape[0] // 3
-    pairs = (
+    copies = (
+        (counts_in, counts),
         (latents, own),
         (w_in, small),
         (gain_in, flat_parts.at[0]),
         (shift_in, flat_parts.at[1]),
         (gain_out, tall_parts.at[0]),
         (shift_out, tall_parts.at[1]),
-        (w_mid, kernel),
-    )
-    loads = [pltpu.make_async_copy(a, b, sems.at[i]) for i, (a, b) in enumerate(pairs)]
+        (w_mid.at[: kernel.shape[0]], kernel),
+    )
+    loads = [pltpu.make_async_copy(a, b, sems.at[i]) for i, (a, b) in enumerate(copies)]
     for load in loads:
         load.start()
     wide[...] = jnp.zeros_like(wide)
@@ -122,7 +154,35 @@
     eye = lax.broadcasted_iota(jnp.int32, (half, half), 0) == lax.broadcasted_iota(
         jnp.int32, (half, half), 1
     )
-    for load in loads[:-1]:
+    block = lax.axis_index("block")
+    find = piece_finder(rows // own_rows, use_ring)
+    loads[0].wait()
+    my_start = jnp.int32(0)
+    for k in range(blocks):
+        my_start = my_start + jnp.where(k < block, counts[k], 0)
+    entries = []
+    for f in range(HALO):
+        wanted = my_start - HALO + f
+        safe = jnp.maximum(wanted, 0)
+        total, begin, owner = jnp.int32(0), jnp.int32(0), jnp.int32(0)
+        for k in range(blocks):
+            total = total + counts[k]
+            past = safe >= total
+            owner = owner + jnp.where(past, 1, 0)
+            begin = jnp.where(past, total, begin)
+        for r in range(rows):
+            piece = find(owner, r // own_rows) * own_rows + r % own_rows
+            entries.append(jnp.where(wanted >= 0, piece * frames + safe - begin, -1))
+    for r in range(rows):
+        piece = find(block, r // own_rows) * own_rows + r % own_rows
+        entries.append(piece * frames)
+    entries += [my_start, counts[block]]
+    lane = lax.broadcasted_iota(jnp.int32, table.shape, 1)
+    line = jnp.zeros(table.shape, jnp.int32)
+    for i, entry in enumerate(entries):
+        line = jnp.where(lane == i, entry, line)
+    table[...] = line
+    for load in loads[1:-1]:
         load.wait()
     for t in range(3):
         for place in range(rows):
@@ -138,8 +198,13 @@
     loads[-1].wait()
 
 
-def prepare(rows, own, w_in, gain_in, shift_in, w_mid, gain_out, shift_out):
-    half = w_mid.shape[4]
+def in_hbm(a):
+    return pltpu.with_memory_space_constraint(a, pltpu.HBM)
+
+
+def prepare(cfg, own, w_in, gain_in, shift_in, gain_out, shift_out, counts, middle):
+    blocks, rows = cfg[:2]
+    half = gain_out.shape[0]
     pairs = -(-rows // 2)
     small = (3, 3, 3 * LAT, C)
     operands = (
@@ -147,53 +212,71 @@
         w_in.reshape(small),
         gain_in,
         shift_in,
-        jnp.transpose(w_mid, (0, 1, 2, 4, 3)).reshape(3, 3, 3 * half, C),
         gain_out,
         shift_out,
+        counts,
+        middle,
     )
     return pl.pallas_call(
-        functools.partial(prepare_body, rows),
+        functools.partial(prepare_body, cfg),
         out_shape=(
             pltpu.VMEM(own.shape, own.dtype),
             pltpu.VMEM((3 * pairs * LANES, rows * C), jnp.bfloat16),
             pltpu.VMEM((C, C), jnp.bfloat16),
-            pltpu.VMEM((3, 3, 3 * half, C), jnp.bfloat16),
             pltpu.VMEM((8, C), jnp.float32),
             pltpu.VMEM((2, half, LANES), jnp.float32),
+            pltpu.VMEM((8, LANES), jnp.int32),
+            pltpu.VMEM((1,) + middle.shape[1:], middle.dtype),
         ),
-        in_specs=[pl.BlockSpec(memory_space=pltpu.HBM)] * 7,
-        out_specs=(pl.BlockSpec(memory_space=pltpu.VMEM),) * 6,
+        in_specs=[pl.BlockSpec(memory_space=pltpu.HBM)] * 8,
+        out_specs=(pl.BlockSpec(memory_space=pltpu.VMEM),) * 7,
         scratch_shapes=[
             pltpu.VMEM(small, jnp.bfloat16),
             pltpu.VMEM((2, C), jnp.float32),
             pltpu.VMEM((2, half), jnp.float32),
-            pltpu.SemaphoreType.DMA((7,)),
+            pltpu.SMEM((blocks,), jnp.int32),
+            pltpu.SemaphoreType.DMA((8,)),
         ],
         compiler_params=pltpu.CompilerParams(vmem_limit_bytes=16 * 1024 * 1024),
-    )(*[pltpu.with_memory_space_constraint(a, pltpu.HBM) for a in operands])
+    )(*[in_hbm(a) for a in operands])
+
+
+def load_body(w_mid, kernel, sem):
+    count = kernel.shape[0]
+    load = pltpu.make_async_copy(w_mid.at[3 - count :], kernel, sem)
+    load.start()
+    load.wait()
+
+
+def load_rest(middle):
+    return pl.pallas_call(
+        load_body,
+        out_shape=pltpu.VMEM((2,) + middle.shape[1:], middle.dtype),
+        in_specs=[pl.BlockSpec(memory_space=pltpu.HBM)],
+        out_specs=pl.BlockSpec(memory_space=pltpu.VMEM),
+        scratch_shapes=[pltpu.SemaphoreType.DMA],
+        compiler_params=pltpu.CompilerParams(vmem_limit_bytes=1024 * 1024),
+    )(in_hbm(middle))
 
 
 def body(cfg, *refs):
-    blocks, rows, frames, columns, pieces, use_ring = cfg
+    rows, frames, columns, pieces = cfg
     n_arrays = len(pieces)
     sources = refs[:n_arrays]
-    (counts_in, wide, matrix, kernel, flat_terms, tall_terms, out) = refs[n_arrays : n_arrays + 7]
-    (counts, slabs, patches, first, acts, second, sem) = refs[n_arrays + 7 :]
+    wide, matrix, flat_terms, tall_terms, table_in, kernel_0, kernel_1, out = refs[
+        n_arrays : n_arrays + 8
+    ]
+    table, slabs, patches, first, acts, second, sem = refs[n_arrays + 8 :]
     half = out.shape[2]
     chunks = columns // COLS_IN_TILE
     slab = -(-(chunks + 1) // 8) * 8
     padded = -(-(columns + 1) // 16) * 16
     stride = -(-(columns + 1) // LANES) * LANES
-    halo = 4
-    lat_frames = frames + halo
+    lat_frames = frames + HALO
     act_frames = frames + 2
     pairs = -(-rows // 2)
-    depth = pairs * LANES
     own_rows = out.shape[1]
-    block = lax.axis_index("block")
-    band = lax.axis_index("band")
-
-    load = pltpu.make_async_copy(counts_in, counts, sem)
+    load = pltpu.make_async_copy(table_in, table, sem)
     load.start()
 
     slabs[...] = jnp.zeros_like(slabs)
@@ -208,40 +291,20 @@
             at += 1
 
     load.wait()
-    my_start = jnp.int32(0)
-    for k in range(blocks):
-        my_start = my_start + jnp.where(k < block, counts[k], 0)
-    my_count = counts[block]
-
+    my_start = table[0, (HALO + 1) * rows]
+    my_count = table[0, (HALO + 1) * rows + 1]
     lane = lax.broadcasted_iota(jnp.int32, (slab, LANES), 1)
     patches[...] = jnp.zeros_like(patches)
     for f in range(lat_frames):
-        if f < halo:
-            wanted = my_start - halo + f
-            valid = wanted >= 0
-            safe = jnp.maximum(wanted, 0)
-            total, begin, owner = jnp.int32(0), jnp.int32(0), jnp.int32(0)
-            for k in range(blocks):
-                total = total + counts[k]
-                past = safe >= total
-                owner = owner + jnp.where(past, 1, 0)
-                begin = jnp.where(past, total, begin)
-            slot = safe - begin
-        else:
-            valid, owner, slot = None, block, jnp.int32(f - halo)
         planes = []
         for r in range(rows):
-            rank, inner = r // own_rows, r % own_rows
-            if use_ring:
-                piece = piece_ring(block, band, owner, rank, blocks)
+            if f < HALO:
+                at = table[0, f * rows + r]
+                top = pl.multiple_of(jnp.maximum(at, 0) * slab, 8)
+                planes.append(jnp.where(at >= 0, slabs[pl.ds(top, slab), :], 0.0))
             else:
-                piece = owner * (rows // own_rows) + rank
-            piece = piece * own_rows + inner
-            top = pl.multiple_of((piece * frames + slot) * slab, 8)
-            plane = slabs[pl.ds(top, slab), :]
-            if valid is not None:
-                plane = jnp.where(valid, plane, 0.0)
-            planes.append(plane)
+                at = table[0, HALO * rows + r] + (f - HALO)
+                planes.append(slabs[pl.ds(pl.multiple_of(at * slab, 8), slab), :])
         if rows % 2:
             planes.append(jnp.zeros_like(planes[0]))
         for g in range(pairs):
@@ -307,6 +370,7 @@
             act = jnp.concatenate([act, jnp.zeros((stride - columns, C), jnp.float32)], axis=0)
             acts[g * stride : (g + 1) * stride, r * C : (r + 1) * C] = act.astype(jnp.bfloat16)
 
+    kernel = [kernel_0.at[0], kernel_1.at[0], kernel_1.at[1]]
     span = frames * stride
     inside = lax.broadcasted_iota(jnp.int32, (half, stride), 1) < columns
     spans = {}
@@ -325,7 +389,7 @@
         weights = jnp.concatenate(
             [
                 jnp.concatenate(
-                    [kernel[t, place - r + 1] for place in places for t in range(3)], axis=1
+                    [kernel[t][place - r + 1] for place in places for t in range(3)], axis=1
                 )
                 for r in members
             ],
@@ -372,7 +436,7 @@
     shift = tall_terms[1] - mean * scale
     for f in range(frames):
         for inner in range(own_rows):
-            part = second[band * own_rows + inner, f]
+            part = second[lax.axis_index("band") * own_rows + inner, f]
             value = silu(part * scale[:, f : f + 1] + shift[:, f : f + 1])
             value = jnp.where(f < my_count, value, 0.0).astype(out.dtype)
             out[f, inner] = value[:, :columns]
@@ -384,13 +448,25 @@
     half = w_mid.shape[4]
     blocks, bands = lax.axis_size("block"), lax.axis_size("band")
     rows = own_rows * bands
-    use_ring = blocks == 4 and bands == 2 and own_rows == 1 and lax.axis_size("chan") == 2
+    use_ring = small_slice(blocks, bands, own_rows, lax.axis_size("chan"))
     own = jnp.transpose(latents, (1, 0, 2))
-    kept, *prepared = prepare(rows, own, w_in, gain_in, shift_in, w_mid, gain_out, shift_out)
+    middle = jnp.transpose(w_mid, (0, 1, 2, 4, 3)).reshape(3, 3, 3 * half, C)
+    kept, *prepared = prepare(
+        (blocks, rows, own_rows, frames, use_ring),
+        own,
+        w_in,
+        gain_in,
+        shift_in,
+        gain_out,
+        shift_out,
+        frame_counts,
+        middle,
+    )
+    prepared.append(load_rest(middle))
     if use_ring:
         sources = exchange_ring(own, kept)
     else:
-        gathered = lax.all_gather(own, ("block", "band"), axis=0)
+        gathered = lax.all_gather(kept, ("block", "band"), axis=0)
         sources = [gathered.reshape(-1, frames, flat)]
     pieces = tuple(a.shape[0] for a in sources)
     chunks = columns // COLS_IN_TILE
@@ -398,27 +474,29 @@
     padded = -(-(columns + 1) // 16) * 16
     stride = -(-(columns + 1) // LANES) * LANES
     pairs = -(-rows // 2)
-    cfg = (blocks, rows, frames, columns, pieces, use_ring)
+    cfg = (rows, frames, columns, pieces)
     vmem = pl.BlockSpec(memory_space=pltpu.VMEM)
     decoded = pl.pallas_call(
         functools.partial(body, cfg),
         out_shape=jax.ShapeDtypeStruct((frames, own_rows, half, columns), jnp.bfloat16),
-        in_specs=[vmem] * len(sources)
-        + [pl.BlockSpec(memory_space=pltpu.HBM)]
-        + [vmem] * 5,
+        in_specs=[vmem] * (len(sources) + len(prepared)),
         out_specs=vmem,
         scratch_shapes=[
-            pltpu.SMEM((blocks,), jnp.int32),
+            pltpu.SMEM((8, LANES), jnp.int32),
             pltpu.VMEM((sum(pieces) * frames * slab, LANES), jnp.float32),
-            pltpu.VMEM((pairs * (frames + 4) * padded, LANES), jnp.float32),
+            pltpu.VMEM((pairs * (frames + HALO) * padded, LANES), jnp.float32),
             pltpu.VMEM(((frames + 2) * padded, rows * C), jnp.float32),
             pltpu.VMEM(((frames + 2) * stride, rows * C), jnp.bfloat16),
             pltpu.VMEM((rows, frames, half, stride), jnp.float32),
             pltpu.SemaphoreType.DMA,
         ],
         compiler_params=pltpu.CompilerParams(vmem_limit_bytes=32 * 1024 * 1024),
-    )(*sources, pltpu.with_memory_space_constraint(frame_counts, pltpu.HBM), *prepared)
+    )(*sources, *prepared)
     return jnp.transpose(decoded, (0, 1, 3, 2))
+
+
+def small_slice(blocks, bands, own_rows, cores):
+    return blocks == 4 and bands == 2 and own_rows == 1 and cores == 2
 
 
 def solution(mesh):

time: 21.5 us -> 19.8 us (0.921)
  starting transfers between devices: 7.31 us -> 5.25 us
  Pallas kernels: 9.11 us -> 10 us
  waiting for transfers between devices: 4.84 us -> 4.11 us
    ppermute x2, starting transfers between devices: 7.3 us -> 5.13 us  [the longest x1 2.97 us: exchange_ring(): first = lax.ppermute(latents, axes, round_moves(FIRST_ROUND))]
    ppermute x1, waiting for transfers between devices: 1.21 us -> 0.01 us  [exchange_ring(): fourth = lax.ppermute(third, axes, swap)]
    pallas_call x1 -> x2, Pallas kernels: 2.39 us -> 3.35 us  [the longest x1 1.76 us: load_rest(): pl.pallas_call(load_body, out_shape=pltpu.VMEM((2,) + middle.shape[1:], m...]
    ppermute x2, waiting for transfers between devices: 3.63 us -> 4.11 us  [the longest x1 2.22 us: exchange_ring(): third = lax.ppermute(held, axes, round_moves(SECOND_ROUND))]
  transfers between devices with their start and end apart: 4 -> 4, of which waited for: 3 -> 2; matrix products, arithmetic and copies ran while one was open for 0% -> 0% of each run, Pallas kernels for 11% -> 17%
where the time goes in v2:
time: 19.8 us; the launch traced here: 19.4 us
  Pallas kernels  10 us (51%)
  starting transfers between devices  5.25 us (27%)
  waiting for transfers between devices  4.11 us (21%)
    pallas_call x1, Pallas kernels, shards(): pl.pallas_call(functools.partial(body, cfg), out_shape=jax.ShapeDtypeStru...  6.64 us
    ppermute x1, starting transfers between devices, exchange_ring(): first = lax.ppermute(latents, axes, round_moves(FIRST_ROUND))  2.97 us
    ppermute x1, waiting for transfers between devices, exchange_ring(): third = lax.ppermute(held, axes, round_moves(SECOND_ROUND))  2.22 us
    ppermute x1, starting transfers between devices, exchange_ring(): third = lax.ppermute(held, axes, round_moves(SECOND_ROUND))  2.16 us
    ppermute x1, waiting for transfers between devices, exchange_ring(): first = lax.ppermute(latents, axes, round_moves(FIRST_ROUND))  1.89 us
    pallas_call x1, Pallas kernels, load_rest(): pl.pallas_call(load_body, out_shape=pltpu.VMEM((2,) + middle.shape[1:], m...  1.76 us
    pallas_call x1, Pallas kernels, prepare(): pl.pallas_call(functools.partial(prepare_body, cfg), out_shape=(pltpu.VME...  1.59 us
  transfers between devices with their start and end apart: 4, of which 2 were waited for; matrix products, arithmetic and copies ran while one was open for 0% of the time, Pallas kernels for 17%

profile of v2, /device:TPU:0, one launch (start us, length us, event | category | flops | bytes accessed | tf_op | source)
XLA Modules:
  0.0 19.4 jit_solution(14640948746668226612)
XLA Ops:
  0.0 3.0 %collective-permute-start = (bf16[1,4,1664]{2,1,0:T(4,128)(2,1)}, bf16[1,4,1664]{2,1,0:T(4,128)(2,1)S(1)}, u32[]{:S(2)}, u32[]{:S(2)}) collective-permute-start(bf16[1,4,1664]{2,1,0:T(4,128)(2,1)} %bitcast.9), channel_id=1, source_target_pairs={{2,0},{0,2},{8,4},{10,6},{4,8},{6,10},{14,12},{12,14},{7,1},{5,3},... | collective-permute-start | bytes 39944 | tf_op jit(solution)/shard_map/ppermute | solution.py:97
  3.0 1.9 %collective-permute-done.refs_1_ = bf16[1,4,1664]{2,1,0:T(4,128)(2,1)S(1)} collective-permute-done((bf16[1,4,1664]{2,1,0:T(4,128)(2,1)}, bf16[1,4,1664]{2,1,0:T(4,128)(2,1)S(1)}, u32[]{:S(2)}, u32[]{:S(2)}) %collective-permute-start) | collective-permute-done | bytes 13344 | tf_op jit(solution)/shard_map/ppermute | solution.py:97
  4.9 0.0 collective-permute-start.1
  4.9 1.6 %shard_map.82 = (bf16[1,4,1664]{2,1,0:T(4,128)(2,1)S(1)}, bf16[384,768]{1,0:T(8,128)(2,1)S(1)}, bf16[384,384]{1,0:T(8,128)(2,1)S(1)}, f32[8,384]{1,0:T(8,128)S(1...) custom-call(bf16[1,4,1664]{2,1,0:T(4,128)(2,1)} %bitcast.10, ...), custom_call_target="tpu_custom_call" | custom-call | tf_op jit(solution)/shard_map/pallas_call | solution.py:220
  6.5 0.0 collective-permute-done.1.refs_2_
  6.5 2.2 %collective-permute-start.2 = (bf16[3,4,1664]{2,1,0:T(4,128)(2,1)S(1)}, bf16[3,4,1664]{2,1,0:T(4,128)(2,1)S(1)}, u32[]{:S(2)}, u32[]{:S(2)}) collective-permute-start(bf16[3,4,1664]{2,1,0:T(4,128)(2,1)S(1)} %shard_map.83), channel_id=1, source_target_pairs={{4,0},{6,2},{0,4},{2,6},{14,8},{12,10},{8,12},{10,14},{5,1},{7,3},... | collective-permute-start | bytes 119816 | tf_op jit(solution)/shard_map/ppermute | solution.py:100
  8.6 2.2 %collective-permute-done.2.refs_3_ = bf16[3,4,1664]{2,1,0:T(4,128)(2,1)S(1)} collective-permute-done((bf16[3,4,1664]{2,1,0:T(4,128)(2,1)S(1)}, bf16[3,4,1664]{2,1,0:T(4,128)(2,1)S(1)}, u32[]{:S(2)}, u32[]{:S(2)}) %collective-permute-start.2) | collective-permute-done | bytes 39968 | tf_op jit(solution)/shard_map/ppermute | solution.py:100
  10.9 0.1 collective-permute-start.3
  11.0 1.8 %shard_map.84.refs_11_ = bf16[2,3,576,384]{3,2,1,0:T(8,128)(2,1)S(1)} custom-call(bf16[3,3,576,384]{3,2,1,0:T(8,128)(2,1)} %bitcast.7), custom_call_target="tpu_custom_call" | custom-call | tf_op jit(solution)/shard_map/pallas_call | solution.py:252
  12.7 0.0 collective-permute-done.3.refs_4_
  12.8 6.6 %shard_map.85 = bf16[4,1,192,104]{3,2,1,0:T(8,128)(2,1)} custom-call(bf16[1,4,1664]{2,1,0:T(4,128)(2,1)S(1)} %get-tuple-element.12.refs_0_, bf16[1,4,1664]{2,1,0:T(4,128)(2,1)S(1)} %collective-permute-done.refs_1_, bf16[1,4,1664]{2,1,0:T(4,128)(2,1)S(1)} %collective-permute-done.1.refs_2_, bf16[3,4,1664]{2,1,0:T(4,128)(2,1)S(1)} %collective-permute-done.2.refs_3_, ...), custom_call_target="tpu_custom_call" | custom-call | tf_op jit(solution)/shard_map/pallas_call | solution.py:479
  (1 shorter events, 0.0 us)
Async XLA Ops:
  0.0 4.9 %collective-permute-start = (bf16[1,4,1664]{2,1,0:T(4,128)(2,1)}, bf16[1,4,1664]{2,1,0:T(4,128)(2,1)S(1)}, u32[]{:S(2)}, u32[]{:S(2)}) collective-permute-start(bf16[1,4,1664]{2,1,0:T(4,128)(2,1)} %bitcast.9), channel_id=1, source_target_pairs={{2,0},{0,2},{8,4},{10,6},{4,8},{6,10},{14,12},{12,14},{7,1},{5,3},... | collective-permute-start | bytes 39944 | tf_op jit(solution)/shard_map/ppermute | solution.py:97
  4.9 1.6 %collective-permute-start.1 = (bf16[1,4,1664]{2,1,0:T(4,128)(2,1)S(1)}, bf16[1,4,1664]{2,1,0:T(4,128)(2,1)S(1)}, u32[]{:S(2)}, u32[]{:S(2)}) collective-permute-start(bf16[1,4,1664]{2,1,0:T(4,128)(2,1)S(1)} %collective-permute-done.refs_1_), channel_id=1, source_target_pairs={{0,1},{1,0},{2,3},{3,2},{4,5},{5,4},{6,7},{7,6},{8,9},{9,8},{10,11... | collective-permute-start | bytes 39944 | tf_op jit(solution)/shard_map/ppermute | solution.py:98
  6.5 4.4 %collective-permute-start.2 = (bf16[3,4,1664]{2,1,0:T(4,128)(2,1)S(1)}, bf16[3,4,1664]{2,1,0:T(4,128)(2,1)S(1)}, u32[]{:S(2)}, u32[]{:S(2)}) collective-permute-start(bf16[3,4,1664]{2,1,0:T(4,128)(2,1)S(1)} %shard_map.83), channel_id=1, source_target_pairs={{4,0},{6,2},{0,4},{2,6},{14,8},{12,10},{8,12},{10,14},{5,1},{7,3},... | collective-permute-start | bytes 119816 | tf_op jit(solution)/shard_map/ppermute | solution.py:100
  10.9 1.9 %collective-permute-start.3 = (bf16[3,4,1664]{2,1,0:T(4,128)(2,1)S(1)}, bf16[3,4,1664]{2,1,0:T(4,128)(2,1)S(1)}, u32[]{:S(2)}, u32[]{:S(2)}) collective-permute-start(bf16[3,4,1664]{2,1,0:T(4,128)(2,1)S(1)} %collective-permute-done.2.refs_3_), channel_id=1, source_target_pairs={{0,1},{1,0},{2,3},{3,2},{4,5},{5,4},{6,7},{7,6},{8,9},{9,8},{10,11... | collective-permute-start | bytes 119816 | tf_op jit(solution)/shard_map/ppermute | solution.py:101

commit v3 on v2

--- a/solution.py
+++ b/solution.py
@@ -196,6 +196,7 @@
         spread = jnp.where(eye, tall_parts[i].reshape(1, half), 0.0)
         tall_terms[i] = jnp.broadcast_to(jnp.sum(spread, axis=1, keepdims=True), (half, LANES))
     loads[-1].wait()
+    differences(rows, kernel.at[0])
 
 
 def in_hbm(a):
@@ -241,21 +242,33 @@
     )(*[in_hbm(a) for a in operands])
 
 
-def load_body(w_mid, kernel, sem):
+def differences(rows, kernel):
+    if rows == 2:
+        kernel[0] = kernel[0] - kernel[1]
+        kernel[2] = kernel[2] - kernel[1]
+
+
+def load_body(rows, w_mid, kernel, sems):
     count = kernel.shape[0]
-    load = pltpu.make_async_copy(w_mid.at[3 - count :], kernel, sem)
-    load.start()
-    load.wait()
-
-
-def load_rest(middle):
+    loads = [
+        pltpu.make_async_copy(w_mid.at[3 - count + i], kernel.at[i], sems.at[i])
+        for i in range(count)
+    ]
+    for load in loads:
+        load.start()
+    for i, load in enumerate(loads):
+        load.wait()
+        differences(rows, kernel.at[i])
+
+
+def load_rest(rows, middle):
     return pl.pallas_call(
-        load_body,
+        functools.partial(load_body, rows),
         out_shape=pltpu.VMEM((2,) + middle.shape[1:], middle.dtype),
         in_specs=[pl.BlockSpec(memory_space=pltpu.HBM)],
         out_specs=pl.BlockSpec(memory_space=pltpu.VMEM),
-        scratch_shapes=[pltpu.SemaphoreType.DMA],
-        compiler_params=pltpu.CompilerParams(vmem_limit_bytes=1024 * 1024),
+        scratch_shapes=[pltpu.SemaphoreType.DMA((2,))],
+        compiler_params=pltpu.CompilerParams(vmem_limit_bytes=4 * 1024 * 1024),
     )(in_hbm(middle))
 
 
@@ -263,10 +276,10 @@
     rows, frames, columns, pieces = cfg
     n_arrays = len(pieces)
     sources = refs[:n_arrays]
-    wide, matrix, flat_terms, tall_terms, table_in, kernel_0, kernel_1, out = refs[
+    wide, matrix, flat_terms, tall_terms, table, kernel_0, kernel_1, out = refs[
         n_arrays : n_arrays + 8
     ]
-    table, slabs, patches, first, acts, second, sem = refs[n_arrays + 8 :]
+    slabs, patches, first, acts, second = refs[n_arrays + 8 :]
     half = out.shape[2]
     chunks = columns // COLS_IN_TILE
     slab = -(-(chunks + 1) // 8) * 8
@@ -276,9 +289,6 @@
     act_frames = frames + 2
     pairs = -(-rows // 2)
     own_rows = out.shape[1]
-    load = pltpu.make_async_copy(table_in, table, sem)
-    load.start()
-
     slabs[...] = jnp.zeros_like(slabs)
     at = 0
     for source, n in zip(sources, pieces):
@@ -290,20 +300,20 @@
                 ]
             at += 1
 
-    load.wait()
-    my_start = table[0, (HALO + 1) * rows]
-    my_count = table[0, (HALO + 1) * rows + 1]
+    line = table[0:1]
+    entry = [line[0, i] for i in range((HALO + 1) * rows + 2)]
+    my_start, my_count = entry[-2:]
     lane = lax.broadcasted_iota(jnp.int32, (slab, LANES), 1)
     patches[...] = jnp.zeros_like(patches)
     for f in range(lat_frames):
         planes = []
         for r in range(rows):
             if f < HALO:
-                at = table[0, f * rows + r]
+                at = entry[f * rows + r]
                 top = pl.multiple_of(jnp.maximum(at, 0) * slab, 8)
                 planes.append(jnp.where(at >= 0, slabs[pl.ds(top, slab), :], 0.0))
             else:
-                at = table[0, HALO * rows + r] + (f - HALO)
+                at = entry[HALO * rows + r] + (f - HALO)
                 planes.append(slabs[pl.ds(pl.multiple_of(at * slab, 8), slab), :])
         if rows % 2:
             planes.append(jnp.zeros_like(planes[0]))
@@ -368,58 +378,61 @@
             part = first[g * padded : g * padded + columns, r * C : (r + 1) * C]
             act = silu(part * scale_g + shift_g)
             act = jnp.concatenate([act, jnp.zeros((stride - columns, C), jnp.float32)], axis=0)
-            acts[g * stride : (g + 1) * stride, r * C : (r + 1) * C] = act.astype(jnp.bfloat16)
+            act = act.astype(jnp.bfloat16)
+            acts[g * stride : (g + 1) * stride, r * C : (r + 1) * C] = act
+            both = act if r == 0 else both + act
+        if rows == 2:
+            acts[g * stride : (g + 1) * stride, 2 * C :] = both
 
     kernel = [kernel_0.at[0], kernel_1.at[0], kernel_1.at[1]]
-    span = frames * stride
     inside = lax.broadcasted_iota(jnp.int32, (half, stride), 1) < columns
-    spans = {}
-    for r in range(rows):
-        spans.setdefault((max(0, r - 1), min(rows - 1, r + 1)), []).append(r)
-    for (low, high), members in spans.items():
-        places = range(low, high + 1)
-        positions = jnp.concatenate(
-            [
-                acts[t * stride : t * stride + span, place * C : (place + 1) * C]
-                for place in places
-                for t in range(3)
-            ],
-            axis=1,
-        )
-        weights = jnp.concatenate(
-            [
-                jnp.concatenate(
-                    [kernel[t][place - r + 1] for place in places for t in range(3)], axis=1
-                )
-                for r in members
-            ],
-            axis=0,
-        )
-        taps = lax.dot_general(
-            weights, positions, (((1,), (1,)), ((), ())), preferred_element_type=jnp.float32
-        )
-        for m, r in enumerate(members):
-            top = m * 3 * half
-            for f in range(frames):
-                left = f * stride
+    lane_at = lax.broadcasted_iota(jnp.int32, (half, LANES), 1)
+    columns_of = jnp.zeros((half, LANES), jnp.float32)
+    group = 2 if frames % 2 == 0 else 1
+    for f0 in range(0, frames, group):
+        span = group * stride
+
+        def product(taps_of, places_of):
+            weights = jnp.concatenate(
+                [kernel[t][y] for y in taps_of for t in range(3)], axis=1
+            )
+            positions = jnp.concatenate(
+                [
+                    acts[(f0 + t) * stride : (f0 + t) * stride + span, p * C : (p + 1) * C]
+                    for p in places_of
+                    for t in range(3)
+                ],
+                axis=1,
+            )
+            return lax.dot_general(
+                weights, positions, (((1,), (1,)), ((), ())), preferred_element_type=jnp.float32
+            )
+
+        if rows == 2:
+            shared = product([1], [2])
+            taps = [shared + product([2], [1]), shared + product([0], [0])]
+        else:
+            taps = []
+            for r in range(rows):
+                places = range(max(0, r - 1), min(rows - 1, r + 1) + 1)
+                taps.append(product([p - r + 1 for p in places], places))
+        for f in range(f0, f0 + group):
+            left = (f - f0) * stride
+            plain = square = jnp.zeros((half, stride), jnp.float32)
+            for r in range(rows):
                 tap = [
-                    taps[top + s * half : top + (s + 1) * half, left : left + stride]
-                    for s in range(3)
+                    taps[r][s * half : (s + 1) * half, left : left + stride] for s in range(3)
                 ]
                 value = tap[1] + pltpu.roll(tap[0], 1, 1) + pltpu.roll(tap[2], stride - 1, 1)
-                second[r, f] = jnp.where(inside, value, 0.0)
-
-    lane_at = lax.broadcasted_iota(jnp.int32, (half, LANES), 1)
-    columns_of = jnp.zeros((half, LANES), jnp.float32)
-    for f in range(frames):
-        plain, square = second[0, f], second[0, f] * second[0, f]
-        for r in range(1, rows):
-            plain = plain + second[r, f]
-            square = square + second[r, f] * second[r, f]
-        columns_of = jnp.where(lane_at == f, jnp.sum(plain, axis=1, keepdims=True), columns_of)
-        columns_of = jnp.where(
-            lane_at == frames + f, jnp.sum(square, axis=1, keepdims=True), columns_of
-        )
+                value = jnp.where(inside, value, 0.0)
+                second[r, f] = value
+                plain = plain + value
+                square = square + value * value
+            columns_of = jnp.where(lane_at == f, jnp.sum(plain, axis=1, keepdims=True), columns_of)
+            columns_of = jnp.where(
+                lane_at == frames + f, jnp.sum(square, axis=1, keepdims=True), columns_of
+            )
+
     high = columns_of.astype(jnp.bfloat16)
     rest = columns_of - high.astype(jnp.float32)
     middle = rest.astype(jnp.bfloat16)
@@ -462,7 +475,7 @@
         frame_counts,
         middle,
     )
-    prepared.append(load_rest(middle))
+    prepared.append(load_rest(rows, middle))
     if use_ring:
         sources = exchange_ring(own, kept)
     else:
@@ -482,13 +495,11 @@
         in_specs=[vmem] * (len(sources) + len(prepared)),
         out_specs=vmem,
         scratch_shapes=[
-            pltpu.SMEM((8, LANES), jnp.int32),
             pltpu.VMEM((sum(pieces) * frames * slab, LANES), jnp.float32),
             pltpu.VMEM((pairs * (frames + HALO) * padded, LANES), jnp.float32),
             pltpu.VMEM(((frames + 2) * padded, rows * C), jnp.float32),
-            pltpu.VMEM(((frames + 2) * stride, rows * C), jnp.bfloat16),
+            pltpu.VMEM(((frames + 2) * stride, (rows + (rows == 2)) * C), jnp.bfloat16),
             pltpu.VMEM((rows, frames, half, stride), jnp.float32),
-            pltpu.SemaphoreType.DMA,
         ],
         compiler_params=pltpu.CompilerParams(vmem_limit_bytes=32 * 1024 * 1024),
     )(*sources, *prepared)

time: 19.8 us -> 18.9 us (0.955)
  Pallas kernels: 10 us -> 9.15 us
    pallas_call x1, Pallas kernels: 6.64 us -> 5.57 us  [shards(): pl.pallas_call(functools.partial(body, cfg), out_shape=jax.ShapeDtypeStru...]
  transfers between devices with their start and end apart: 4 -> 4, of which waited for: 2 -> 2; matrix products, arithmetic and copies ran while one was open for 0% -> 0% of each run, Pallas kernels for 17% -> 19%
where the time goes in v3:
time: 18.9 us; the launch traced here: 18.6 us
  Pallas kernels  9.15 us (48%)
  starting transfers between devices  5.25 us (28%)
  waiting for transfers between devices  4.11 us (22%)
    pallas_call x1, Pallas kernels, shards(): pl.pallas_call(functools.partial(body, cfg), out_shape=jax.ShapeDtypeStru...  5.57 us
    ppermute x1, starting transfers between devices, exchange_ring(): first = lax.ppermute(latents, axes, round_moves(FIRST_ROUND))  2.97 us
    ppermute x1, waiting for transfers between devices, exchange_ring(): third = lax.ppermute(held, axes, round_moves(SECOND_ROUND))  2.22 us
    ppermute x1, starting transfers between devices, exchange_ring(): third = lax.ppermute(held, axes, round_moves(SECOND_ROUND))  2.16 us
    ppermute x1, waiting for transfers between devices, exchange_ring(): first = lax.ppermute(latents, axes, round_moves(FIRST_ROUND))  1.89 us
    pallas_call x1, Pallas kernels, load_rest(): pl.pallas_call(functools.partial(load_body, rows), out_shape=pltpu.VMEM((...  1.86 us
    pallas_call x1, Pallas kernels, prepare(): pl.pallas_call(functools.partial(prepare_body, cfg), out_shape=(pltpu.VME...  1.72 us
  transfers between devices with their start and end apart: 4, of which 2 were waited for; matrix products, arithmetic and copies ran while one was open for 0% of the time, Pallas kernels for 19%

profile of v3, /device:TPU:0, one launch (start us, length us, event | category | flops | bytes accessed | tf_op | source)
XLA Modules:
  0.0 18.6 jit_solution(6816021480628144944)
XLA Ops:
  0.0 3.0 %collective-permute-start = (bf16[1,4,1664]{2,1,0:T(4,128)(2,1)}, bf16[1,4,1664]{2,1,0:T(4,128)(2,1)S(1)}, u32[]{:S(2)}, u32[]{:S(2)}) collective-permute-start(bf16[1,4,1664]{2,1,0:T(4,128)(2,1)} %bitcast.9), channel_id=1, source_target_pairs={{2,0},{0,2},{8,4},{10,6},{4,8},{6,10},{14,12},{12,14},{7,1},{5,3},... | collective-permute-start | bytes 39944 | tf_op jit(solution)/shard_map/ppermute | solution.py:97
  3.0 1.9 %collective-permute-done.refs_1_ = bf16[1,4,1664]{2,1,0:T(4,128)(2,1)S(1)} collective-permute-done((bf16[1,4,1664]{2,1,0:T(4,128)(2,1)}, bf16[1,4,1664]{2,1,0:T(4,128)(2,1)S(1)}, u32[]{:S(2)}, u32[]{:S(2)}) %collective-permute-start) | collective-permute-done | bytes 13344 | tf_op jit(solution)/shard_map/ppermute | solution.py:97
  4.9 0.0 collective-permute-start.1
  4.9 1.7 %shard_map.82 = (bf16[1,4,1664]{2,1,0:T(4,128)(2,1)S(1)}, bf16[384,768]{1,0:T(8,128)(2,1)S(1)}, bf16[384,384]{1,0:T(8,128)(2,1)S(1)}, f32[8,384]{1,0:T(8,128)S(1...) custom-call(bf16[1,4,1664]{2,1,0:T(4,128)(2,1)} %bitcast.10, ...), custom_call_target="tpu_custom_call" | custom-call | tf_op jit(solution)/shard_map/pallas_call | solution.py:221
  6.6 0.0 collective-permute-done.1.refs_2_
  6.6 2.2 %collective-permute-start.2 = (bf16[3,4,1664]{2,1,0:T(4,128)(2,1)S(1)}, bf16[3,4,1664]{2,1,0:T(4,128)(2,1)S(1)}, u32[]{:S(2)}, u32[]{:S(2)}) collective-permute-start(bf16[3,4,1664]{2,1,0:T(4,128)(2,1)S(1)} %shard_map.83), channel_id=1, source_target_pairs={{4,0},{6,2},{0,4},{2,6},{14,8},{12,10},{8,12},{10,14},{5,1},{7,3},... | collective-permute-start | bytes 119816 | tf_op jit(solution)/shard_map/ppermute | solution.py:100
  8.8 2.2 %collective-permute-done.2.refs_3_ = bf16[3,4,1664]{2,1,0:T(4,128)(2,1)S(1)} collective-permute-done((bf16[3,4,1664]{2,1,0:T(4,128)(2,1)S(1)}, bf16[3,4,1664]{2,1,0:T(4,128)(2,1)S(1)}, u32[]{:S(2)}, u32[]{:S(2)}) %collective-permute-start.2) | collective-permute-done | bytes 39968 | tf_op jit(solution)/shard_map/ppermute | solution.py:100
  11.0 0.1 collective-permute-start.3
  11.1 1.9 %shard_map.84.refs_11_ = bf16[2,3,576,384]{3,2,1,0:T(8,128)(2,1)S(1)} custom-call(bf16[3,3,576,384]{3,2,1,0:T(8,128)(2,1)} %bitcast.7), custom_call_target="tpu_custom_call" | custom-call | tf_op jit(solution)/shard_map/pallas_call | solution.py:265
  13.0 0.0 collective-permute-done.3.refs_4_
  13.0 5.6 %shard_map.85 = bf16[4,1,192,104]{3,2,1,0:T(8,128)(2,1)} custom-call(bf16[1,4,1664]{2,1,0:T(4,128)(2,1)S(1)} %get-tuple-element.12.refs_0_, bf16[1,4,1664]{2,1,0:T(4,128)(2,1)S(1)} %collective-permute-done.refs_1_, bf16[1,4,1664]{2,1,0:T(4,128)(2,1)S(1)} %collective-permute-done.1.refs_2_, bf16[3,4,1664]{2,1,0:T(4,128)(2,1)S(1)} %collective-permute-done.2.refs_3_, ...), custom_call_target="tpu_custom_call" | custom-call | tf_op jit(solution)/shard_map/pallas_call | solution.py:492
  (1 shorter events, 0.0 us)
Async XLA Ops:
  0.0 4.9 %collective-permute-start = (bf16[1,4,1664]{2,1,0:T(4,128)(2,1)}, bf16[1,4,1664]{2,1,0:T(4,128)(2,1)S(1)}, u32[]{:S(2)}, u32[]{:S(2)}) collective-permute-start(bf16[1,4,1664]{2,1,0:T(4,128)(2,1)} %bitcast.9), channel_id=1, source_target_pairs={{2,0},{0,2},{8,4},{10,6},{4,8},{6,10},{14,12},{12,14},{7,1},{5,3},... | collective-permute-start | bytes 39944 | tf_op jit(solution)/shard_map/ppermute | solution.py:97
  4.9 1.7 %collective-permute-start.1 = (bf16[1,4,1664]{2,1,0:T(4,128)(2,1)S(1)}, bf16[1,4,1664]{2,1,0:T(4,128)(2,1)S(1)}, u32[]{:S(2)}, u32[]{:S(2)}) collective-permute-start(bf16[1,4,1664]{2,1,0:T(4,128)(2,1)S(1)} %collective-permute-done.refs_1_), channel_id=1, source_target_pairs={{0,1},{1,0},{2,3},{3,2},{4,5},{5,4},{6,7},{7,6},{8,9},{9,8},{10,11... | collective-permute-start | bytes 39944 | tf_op jit(solution)/shard_map/ppermute | solution.py:98
  6.6 4.4 %collective-permute-start.2 = (bf16[3,4,1664]{2,1,0:T(4,128)(2,1)S(1)}, bf16[3,4,1664]{2,1,0:T(4,128)(2,1)S(1)}, u32[]{:S(2)}, u32[]{:S(2)}) collective-permute-start(bf16[3,4,1664]{2,1,0:T(4,128)(2,1)S(1)} %shard_map.83), channel_id=1, source_target_pairs={{4,0},{6,2},{0,4},{2,6},{14,8},{12,10},{8,12},{10,14},{5,1},{7,3},... | collective-permute-start | bytes 119816 | tf_op jit(solution)/shard_map/ppermute | solution.py:100
  11.0 2.0 %collective-permute-start.3 = (bf16[3,4,1664]{2,1,0:T(4,128)(2,1)S(1)}, bf16[3,4,1664]{2,1,0:T(4,128)(2,1)S(1)}, u32[]{:S(2)}, u32[]{:S(2)}) collective-permute-start(bf16[3,4,1664]{2,1,0:T(4,128)(2,1)S(1)} %collective-permute-done.2.refs_3_), channel_id=1, source_target_pairs={{0,1},{1,0},{2,3},{3,2},{4,5},{5,4},{6,7},{7,6},{8,9},{9,8},{10,11... | collective-permute-start | bytes 119816 | tf_op jit(solution)/shard_map/ppermute | solution.py:101

commit v4 on v3

--- a/solution.py
+++ b/solution.py
@@ -121,9 +121,43 @@
     return out[:rows] + out[rows : 2 * rows] + out[2 * rows :]
 
 
-def silu(u):
-    half_u = 0.5 * u
-    return half_u + half_u * jnp.tanh(half_u)
+def half_silu(h):
+    return h + h * jnp.tanh(h)
+
+
+def group_columns(values, size):
+    row = lax.broadcasted_iota(jnp.int32, (8, LANES), 0)
+    groups = []
+    for top in range(0, values.shape[0], 2 * WIDTH):
+        a, b, c = (values[top + 8 * i : top + 8 * (i + 1)] for i in range(3))
+        groups.append(a + jnp.where(row < 4, b, 0.0))
+        groups.append(c + jnp.where(row < 4, 0.0, b))
+    groups += [jnp.zeros((8, LANES), jnp.float32)] * (-len(groups) % 8)
+    out = []
+    for at in range(0, len(groups), 8):
+        tiles = groups[at : at + 8]
+        for step in (4, 2, 1):
+            first_half = (row & step) == 0
+            tiles = [
+                jnp.where(first_half, x, y)
+                + jnp.where(first_half, pltpu.roll(x, 8 - step, 0), pltpu.roll(y, step, 0))
+                for x, y in zip(tiles[::2], tiles[1::2])
+            ]
+        out.append(jnp.sum(tiles[0], axis=1, keepdims=True) / size)
+    return out
+
+
+def group_rows(tiles, rows, lanes):
+    row = lax.broadcasted_iota(jnp.int32, (8, lanes), 0)
+    spread = []
+    for n in range(rows // WIDTH):
+        j = n % 8
+        at = (j & 1) * 4 + (j & 2) + (j >> 2)
+        spread.append(jnp.broadcast_to(tiles[n // 8][at : at + 1, :], (8, lanes)))
+    out = []
+    for a, b in zip(spread[::2], spread[1::2]):
+        out += [a, jnp.where(row < 4, a, b), b]
+    return jnp.concatenate(out, axis=0)
 
 
 HALO = 4
@@ -192,8 +226,8 @@
                     top = t * depth + place * 64
                     wide[top : top + 3 * LAT, r * C : (r + 1) * C] = small[t, y]
     for i in range(2):
-        flat_terms[i : i + 1] = flat_parts[i].reshape(1, C)
-        spread = jnp.where(eye, tall_parts[i].reshape(1, half), 0.0)
+        flat_terms[i : i + 1] = 0.5 * flat_parts[i].reshape(1, C)
+        spread = jnp.where(eye, 0.5 * tall_parts[i].reshape(1, half), 0.0)
         tall_terms[i] = jnp.broadcast_to(jnp.sum(spread, axis=1, keepdims=True), (half, LANES))
     loads[-1].wait()
     differences(rows, kernel.at[0])
@@ -279,17 +313,15 @@
     wide, matrix, flat_terms, tall_terms, table, kernel_0, kernel_1, out = refs[
         n_arrays : n_arrays + 8
     ]
-    slabs, patches, first, acts, second = refs[n_arrays + 8 :]
+    slabs, patches, first, acts = refs[n_arrays + 8 :]
     half = out.shape[2]
     chunks = columns // COLS_IN_TILE
     slab = -(-(chunks + 1) // 8) * 8
     padded = -(-(columns + 1) // 16) * 16
     stride = -(-(columns + 1) // LANES) * LANES
     lat_frames = frames + HALO
-    act_frames = frames + 2
     pairs = -(-rows // 2)
     own_rows = out.shape[1]
-    slabs[...] = jnp.zeros_like(slabs)
     at = 0
     for source, n in zip(sources, pieces):
         for p in range(n):
@@ -298,13 +330,20 @@
                 slabs[pl.ds(at * frames * slab + b, frames, stride=slab), :] = values[
                     :, b * LANES : (b + 1) * LANES
                 ]
+            for b in range(chunks, slab):
+                slabs[pl.ds(at * frames * slab + b, frames, stride=slab), :] = jnp.zeros(
+                    (frames, LANES), jnp.float32
+                )
             at += 1
 
     line = table[0:1]
     entry = [line[0, i] for i in range((HALO + 1) * rows + 2)]
     my_start, my_count = entry[-2:]
     lane = lax.broadcasted_iota(jnp.int32, (slab, LANES), 1)
-    patches[...] = jnp.zeros_like(patches)
+    for i in range(pairs * lat_frames):
+        patches[i * padded + columns : (i + 1) * padded] = jnp.zeros(
+            (padded - columns, LANES), jnp.float32
+        )
     for f in range(lat_frames):
         planes = []
         for r in range(rows):
@@ -343,116 +382,124 @@
                 ] = mixed[:chunks]
 
     low_patches = patches[...].astype(jnp.bfloat16)
-    stacked = jnp.concatenate(
-        [
-            low_patches[(g * lat_frames + t) * padded : (g * lat_frames + t + act_frames) * padded]
-            for t in range(3)
-            for g in range(pairs)
-        ],
-        axis=1,
-    )
-    first[...] = jnp.dot(stacked, wide[...], preferred_element_type=jnp.float32)
-
-    sums, squares = [], []
-    for g in range(act_frames):
-        plain = jnp.zeros((1, C), jnp.float32)
-        square = jnp.zeros((1, C), jnp.float32)
-        for r in range(rows):
-            part = first[g * padded : (g + 1) * padded, r * C : (r + 1) * C]
-            plain = plain + jnp.sum(part, axis=0, keepdims=True)
-            square = square + jnp.sum(part * part, axis=0, keepdims=True)
-        sums.append(plain)
-        squares.append(square)
-    fill = [jnp.zeros((1, C), jnp.float32)] * (-(2 * act_frames) % 16)
-    totals = group_sums(jnp.concatenate(sums + squares + fill, axis=0), matrix[...])
     size = float(rows * columns * WIDTH)
-    mean = totals[:act_frames] / size
-    variance = totals[act_frames : 2 * act_frames] / size - mean * mean
-    scale = lax.rsqrt(variance + EPSILON) * flat_terms[0:1]
-    shift = flat_terms[1:2] - mean * scale
-    for g in range(act_frames):
-        live = my_start - 2 + g >= 0
-        scale_g = jnp.where(live, scale[g : g + 1], 0.0)
-        shift_g = jnp.where(live, shift[g : g + 1], 0.0)
-        for r in range(rows):
-            part = first[g * padded : g * padded + columns, r * C : (r + 1) * C]
-            act = silu(part * scale_g + shift_g)
-            act = jnp.concatenate([act, jnp.zeros((stride - columns, C), jnp.float32)], axis=0)
-            act = act.astype(jnp.bfloat16)
-            acts[g * stride : (g + 1) * stride, r * C : (r + 1) * C] = act
-            both = act if r == 0 else both + act
-        if rows == 2:
-            acts[g * stride : (g + 1) * stride, 2 * C :] = both
+
+    def front(g0, g1):
+        stacked = jnp.concatenate(
+            [
+                low_patches[
+                    (g * lat_frames + t + g0) * padded : (g * lat_frames + t + g1) * padded
+                ]
+                for t in range(3)
+                for g in range(pairs)
+            ],
+            axis=1,
+        )
+        first[g0 * padded : g1 * padded] = jnp.dot(
+            stacked, wide[...], preferred_element_type=jnp.float32
+        )
+        sums, squares = [], []
+        for g in range(g0, g1):
+            plain = jnp.zeros((1, C), jnp.float32)
+            square = jnp.zeros((1, C), jnp.float32)
+            for r in range(rows):
+                part = first[g * padded : (g + 1) * padded, r * C : (r + 1) * C]
+                plain = plain + jnp.sum(part, axis=0, keepdims=True)
+                square = square + jnp.sum(part * part, axis=0, keepdims=True)
+            sums.append(plain)
+            squares.append(square)
+        n = g1 - g0
+        fill = [jnp.zeros((1, C), jnp.float32)] * (-(2 * n) % 16)
+        totals = group_sums(jnp.concatenate(sums + squares + fill, axis=0), matrix[...])
+        mean = totals[:n] / size
+        variance = totals[n : 2 * n] / size - mean * mean
+        scale = lax.rsqrt(variance + EPSILON) * flat_terms[0:1]
+        shift = flat_terms[1:2] - mean * scale
+        for g in range(g0, g1):
+            scale_g, shift_g = scale[g - g0 : g - g0 + 1], shift[g - g0 : g - g0 + 1]
+            if g < 2:
+                live = my_start - 2 + g >= 0
+                scale_g, shift_g = jnp.where(live, scale_g, 0.0), jnp.where(live, shift_g, 0.0)
+            for r in range(rows):
+                part = first[g * padded : g * padded + columns, r * C : (r + 1) * C]
+                act = half_silu(part * scale_g + shift_g)
+                act = jnp.concatenate([act, jnp.zeros((stride - columns, C), jnp.float32)], axis=0)
+                act = act.astype(jnp.bfloat16)
+                acts[g * stride : (g + 1) * stride, r * C : (r + 1) * C] = act
+                both = act if r == 0 else both + act
+            if rows == 2:
+                acts[g * stride : (g + 1) * stride, 2 * C :] = both
 
     kernel = [kernel_0.at[0], kernel_1.at[0], kernel_1.at[1]]
     inside = lax.broadcasted_iota(jnp.int32, (half, stride), 1) < columns
-    lane_at = lax.broadcasted_iota(jnp.int32, (half, LANES), 1)
-    columns_of = jnp.zeros((half, LANES), jnp.float32)
     group = 2 if frames % 2 == 0 else 1
-    for f0 in range(0, frames, group):
-        span = group * stride
-
-        def product(taps_of, places_of):
-            weights = jnp.concatenate(
-                [kernel[t][y] for y in taps_of for t in range(3)], axis=1
-            )
-            positions = jnp.concatenate(
-                [
-                    acts[(f0 + t) * stride : (f0 + t) * stride + span, p * C : (p + 1) * C]
-                    for p in places_of
-                    for t in range(3)
-                ],
-                axis=1,
-            )
-            return lax.dot_general(
-                weights, positions, (((1,), (1,)), ((), ())), preferred_element_type=jnp.float32
-            )
-
+    span = group * stride
+
+    def terms(y, place):
+        return [(y, place, t, c) for t in range(3) for c in range(C // LANES)]
+
+    def product(f0, parts):
+        weights = jnp.concatenate(
+            [kernel[t][y][:, c * LANES : (c + 1) * LANES] for y, _, t, c in parts], axis=1
+        )
+        positions = jnp.concatenate(
+            [
+                acts[
+                    (f0 + t) * stride : (f0 + t) * stride + span,
+                    p * C + c * LANES : p * C + (c + 1) * LANES,
+                ]
+                for _, p, t, c in parts
+            ],
+            axis=1,
+        )
+        return lax.dot_general(
+            weights, positions, (((1,), (1,)), ((), ())), preferred_element_type=jnp.float32
+        )
+
+    def back(f0):
         if rows == 2:
-            shared = product([1], [2])
-            taps = [shared + product([2], [1]), shared + product([0], [0])]
+            middle = terms(1, 2)
+            keep = len(middle) // 2 * 2
+            shared = product(f0, middle[:keep])
+            taps = [
+                shared + product(f0, terms(2, 1) + middle[keep:]),
+                shared + product(f0, terms(0, 0) + middle[keep:]),
+            ]
         else:
             taps = []
             for r in range(rows):
                 places = range(max(0, r - 1), min(rows - 1, r + 1) + 1)
-                taps.append(product([p - r + 1 for p in places], places))
-        for f in range(f0, f0 + group):
-            left = (f - f0) * stride
+                taps.append(product(f0, [q for p in places for q in terms(p - r + 1, p)]))
+        band = lax.axis_index("band")
+        for i in range(group):
             plain = square = jnp.zeros((half, stride), jnp.float32)
+            own = [jnp.zeros((half, stride), jnp.float32)] * own_rows
             for r in range(rows):
                 tap = [
-                    taps[r][s * half : (s + 1) * half, left : left + stride] for s in range(3)
+                    taps[r][s * half : (s + 1) * half, i * stride : (i + 1) * stride]
+                    for s in range(3)
                 ]
                 value = tap[1] + pltpu.roll(tap[0], 1, 1) + pltpu.roll(tap[2], stride - 1, 1)
                 value = jnp.where(inside, value, 0.0)
-                second[r, f] = value
                 plain = plain + value
                 square = square + value * value
-            columns_of = jnp.where(lane_at == f, jnp.sum(plain, axis=1, keepdims=True), columns_of)
-            columns_of = jnp.where(
-                lane_at == frames + f, jnp.sum(square, axis=1, keepdims=True), columns_of
-            )
-
-    high = columns_of.astype(jnp.bfloat16)
-    rest = columns_of - high.astype(jnp.float32)
-    middle = rest.astype(jnp.bfloat16)
-    low = (rest - middle.astype(jnp.float32)).astype(jnp.bfloat16)
-    matrix2 = matrix[:half, :half]
-    totals = (
-        jnp.dot(matrix2, high, preferred_element_type=jnp.float32)
-        + jnp.dot(matrix2, middle, preferred_element_type=jnp.float32)
-        + jnp.dot(matrix2, low, preferred_element_type=jnp.float32)
-    )
-    mean = totals / size
-    variance = pltpu.roll(mean, LANES - frames, 1) - mean * mean
-    scale = lax.rsqrt(variance + EPSILON) * tall_terms[0]
-    shift = tall_terms[1] - mean * scale
-    for f in range(frames):
-        for inner in range(own_rows):
-            part = second[lax.axis_index("band") * own_rows + inner, f]
-            value = silu(part * scale[:, f : f + 1] + shift[:, f : f + 1])
-            value = jnp.where(f < my_count, value, 0.0).astype(out.dtype)
-            out[f, inner] = value[:, :columns]
+                own = [
+                    value if r == 0 else jnp.where(band * own_rows + inner == r, value, own[inner])
+                    for inner in range(own_rows)
+                ]
+            mean = group_columns(plain, size)
+            power = group_columns(square, size)
+            inverse = [lax.rsqrt(p - m * m + EPSILON) for p, m in zip(power, mean)]
+            scale = group_rows(inverse, half, stride) * tall_terms[0]
+            shift = tall_terms[1] - group_rows(mean, half, stride) * scale
+            for inner in range(own_rows):
+                value = half_silu(own[inner] * scale + shift)
+                value = jnp.where(f0 + i < my_count, value, 0.0).astype(out.dtype)
+                out[f0 + i, inner] = value[:, :columns]
+
+    front(0, frames + 2)
+    for f0 in range(0, frames, group):
+        back(f0)
 
 
 def shards(latents, frame_counts, w_in, gain_in, shift_in, w_mid, gain_out, shift_out):
@@ -499,7 +546,6 @@
             pltpu.VMEM((pairs * (frames + HALO) * padded, LANES), jnp.float32),
             pltpu.VMEM(((frames + 2) * padded, rows * C), jnp.float32),
             pltpu.VMEM(((frames + 2) * stride, (rows + (rows == 2)) * C), jnp.bfloat16),
-            pltpu.VMEM((rows, frames, half, stride), jnp.float32),
         ],
         compiler_params=pltpu.CompilerParams(vmem_limit_bytes=32 * 1024 * 1024),
     )(*sources, *prepared)

time: 18.9 us -> 18.1 us (0.958)
  Pallas kernels: 9.15 us -> 8.39 us
    pallas_call x1, Pallas kernels: 5.57 us -> 4.81 us  [shards(): pl.pallas_call(functools.partial(body, cfg), out_shape=jax.ShapeDtypeStru...]
  transfers between devices with their start and end apart: 4 -> 4, of which waited for: 2 -> 2; matrix products, arithmetic and copies ran while one was open for 0% -> 0% of each run, Pallas kernels for 19% -> 20%
where the time goes in v4:
time: 18.1 us; the launch traced here: 17.8 us
  Pallas kernels  8.39 us (46%)
  starting transfers between devices  5.25 us (29%)
  waiting for transfers between devices  4.11 us (23%)
    pallas_call x1, Pallas kernels, shards(): pl.pallas_call(functools.partial(body, cfg), out_shape=jax.ShapeDtypeStru...  4.81 us
    ppermute x1, starting transfers between devices, exchange_ring(): first = lax.ppermute(latents, axes, round_moves(FIRST_ROUND))  2.97 us
    ppermute x1, waiting for transfers between devices, exchange_ring(): third = lax.ppermute(held, axes, round_moves(SECOND_ROUND))  2.22 us
    ppermute x1, starting transfers between devices, exchange_ring(): third = lax.ppermute(held, axes, round_moves(SECOND_ROUND))  2.16 us
    ppermute x1, waiting for transfers between devices, exchange_ring(): first = lax.ppermute(latents, axes, round_moves(FIRST_ROUND))  1.89 us
    pallas_call x1, Pallas kernels, load_rest(): pl.pallas_call(functools.partial(load_body, rows), out_shape=pltpu.VMEM((...  1.86 us
    pallas_call x1, Pallas kernels, prepare(): pl.pallas_call(functools.partial(prepare_body, cfg), out_shape=(pltpu.VME...  1.72 us
  transfers between devices with their start and end apart: 4, of which 2 were waited for; matrix products, arithmetic and copies ran while one was open for 0% of the time, Pallas kernels for 20%

profile of v4, /device:TPU:0, one launch (start us, length us, event | category | flops | bytes accessed | tf_op | source)
XLA Modules:
  0.0 17.8 jit_solution(9359376199223882885)
XLA Ops:
  0.0 3.0 %collective-permute-start = (bf16[1,4,1664]{2,1,0:T(4,128)(2,1)}, bf16[1,4,1664]{2,1,0:T(4,128)(2,1)S(1)}, u32[]{:S(2)}, u32[]{:S(2)}) collective-permute-start(bf16[1,4,1664]{2,1,0:T(4,128)(2,1)} %bitcast.9), channel_id=1, source_target_pairs={{2,0},{0,2},{8,4},{10,6},{4,8},{6,10},{14,12},{12,14},{7,1},{5,3},... | collective-permute-start | bytes 39944 | tf_op jit(solution)/shard_map/ppermute | solution.py:97
  3.0 1.9 %collective-permute-done.refs_1_ = bf16[1,4,1664]{2,1,0:T(4,128)(2,1)S(1)} collective-permute-done((bf16[1,4,1664]{2,1,0:T(4,128)(2,1)}, bf16[1,4,1664]{2,1,0:T(4,128)(2,1)S(1)}, u32[]{:S(2)}, u32[]{:S(2)}) %collective-permute-start) | collective-permute-done | bytes 13344 | tf_op jit(solution)/shard_map/ppermute | solution.py:97
  4.9 0.0 collective-permute-start.1
  4.9 1.7 %shard_map.82 = (bf16[1,4,1664]{2,1,0:T(4,128)(2,1)S(1)}, bf16[384,768]{1,0:T(8,128)(2,1)S(1)}, bf16[384,384]{1,0:T(8,128)(2,1)S(1)}, f32[8,384]{1,0:T(8,128)S(1...) custom-call(bf16[1,4,1664]{2,1,0:T(4,128)(2,1)} %bitcast.10, ...), custom_call_target="tpu_custom_call" | custom-call | tf_op jit(solution)/shard_map/pallas_call | solution.py:255
  6.6 0.0 collective-permute-done.1.refs_2_
  6.6 2.2 %collective-permute-start.2 = (bf16[3,4,1664]{2,1,0:T(4,128)(2,1)S(1)}, bf16[3,4,1664]{2,1,0:T(4,128)(2,1)S(1)}, u32[]{:S(2)}, u32[]{:S(2)}) collective-permute-start(bf16[3,4,1664]{2,1,0:T(4,128)(2,1)S(1)} %shard_map.83), channel_id=1, source_target_pairs={{4,0},{6,2},{0,4},{2,6},{14,8},{12,10},{8,12},{10,14},{5,1},{7,3},... | collective-permute-start | bytes 119816 | tf_op jit(solution)/shard_map/ppermute | solution.py:100
  8.8 2.2 %collective-permute-done.2.refs_3_ = bf16[3,4,1664]{2,1,0:T(4,128)(2,1)S(1)} collective-permute-done((bf16[3,4,1664]{2,1,0:T(4,128)(2,1)S(1)}, bf16[3,4,1664]{2,1,0:T(4,128)(2,1)S(1)}, u32[]{:S(2)}, u32[]{:S(2)}) %collective-permute-start.2) | collective-permute-done | bytes 39968 | tf_op jit(solution)/shard_map/ppermute | solution.py:100
  11.0 0.1 collective-permute-start.3
  11.1 1.9 %shard_map.84.refs_11_ = bf16[2,3,576,384]{3,2,1,0:T(8,128)(2,1)S(1)} custom-call(bf16[3,3,576,384]{3,2,1,0:T(8,128)(2,1)} %bitcast.7), custom_call_target="tpu_custom_call" | custom-call | tf_op jit(solution)/shard_map/pallas_call | solution.py:299
  13.0 0.0 collective-permute-done.3.refs_4_
  13.0 4.8 %shard_map.85 = bf16[4,1,192,104]{3,2,1,0:T(8,128)(2,1)} custom-call(bf16[1,4,1664]{2,1,0:T(4,128)(2,1)S(1)} %get-tuple-element.12.refs_0_, bf16[1,4,1664]{2,1,0:T(4,128)(2,1)S(1)} %collective-permute-done.refs_1_, bf16[1,4,1664]{2,1,0:T(4,128)(2,1)S(1)} %collective-permute-done.1.refs_2_, bf16[3,4,1664]{2,1,0:T(4,128)(2,1)S(1)} %collective-permute-done.2.refs_3_, ...), custom_call_target="tpu_custom_call" | custom-call | tf_op jit(solution)/shard_map/pallas_call | solution.py:539
  (1 shorter events, 0.0 us)
Async XLA Ops:
  0.0 4.9 %collective-permute-start = (bf16[1,4,1664]{2,1,0:T(4,128)(2,1)}, bf16[1,4,1664]{2,1,0:T(4,128)(2,1)S(1)}, u32[]{:S(2)}, u32[]{:S(2)}) collective-permute-start(bf16[1,4,1664]{2,1,0:T(4,128)(2,1)} %bitcast.9), channel_id=1, source_target_pairs={{2,0},{0,2},{8,4},{10,6},{4,8},{6,10},{14,12},{12,14},{7,1},{5,3},... | collective-permute-start | bytes 39944 | tf_op jit(solution)/shard_map/ppermute | solution.py:97
  4.9 1.7 %collective-permute-start.1 = (bf16[1,4,1664]{2,1,0:T(4,128)(2,1)S(1)}, bf16[1,4,1664]{2,1,0:T(4,128)(2,1)S(1)}, u32[]{:S(2)}, u32[]{:S(2)}) collective-permute-start(bf16[1,4,1664]{2,1,0:T(4,128)(2,1)S(1)} %collective-permute-done.refs_1_), channel_id=1, source_target_pairs={{0,1},{1,0},{2,3},{3,2},{4,5},{5,4},{6,7},{7,6},{8,9},{9,8},{10,11... | collective-permute-start | bytes 39944 | tf_op jit(solution)/shard_map/ppermute | solution.py:98
  6.6 4.4 %collective-permute-start.2 = (bf16[3,4,1664]{2,1,0:T(4,128)(2,1)S(1)}, bf16[3,4,1664]{2,1,0:T(4,128)(2,1)S(1)}, u32[]{:S(2)}, u32[]{:S(2)}) collective-permute-start(bf16[3,4,1664]{2,1,0:T(4,128)(2,1)S(1)} %shard_map.83), channel_id=1, source_target_pairs={{4,0},{6,2},{0,4},{2,6},{14,8},{12,10},{8,12},{10,14},{5,1},{7,3},... | collective-permute-start | bytes 119816 | tf_op jit(solution)/shard_map/ppermute | solution.py:100
  11.0 2.0 %collective-permute-start.3 = (bf16[3,4,1664]{2,1,0:T(4,128)(2,1)S(1)}, bf16[3,4,1664]{2,1,0:T(4,128)(2,1)S(1)}, u32[]{:S(2)}, u32[]{:S(2)}) collective-permute-start(bf16[3,4,1664]{2,1,0:T(4,128)(2,1)S(1)} %collective-permute-done.2.refs_3_), channel_id=1, source_target_pairs={{0,1},{1,0},{2,3},{3,2},{4,5},{5,4},{6,7},{7,6},{8,9},{9,8},{10,11... | collective-permute-start | bytes 119816 | tf_op jit(solution)/shard_map/ppermute | solution.py:101

commit v5 on v4

--- a/solution.py
+++ b/solution.py
@@ -400,12 +400,14 @@
         )
         sums, squares = [], []
         for g in range(g0, g1):
-            plain = jnp.zeros((1, C), jnp.float32)
-            square = jnp.zeros((1, C), jnp.float32)
+            plain = square = jnp.zeros((8, C), jnp.float32)
             for r in range(rows):
-                part = first[g * padded : (g + 1) * padded, r * C : (r + 1) * C]
-                plain = plain + jnp.sum(part, axis=0, keepdims=True)
-                square = square + jnp.sum(part * part, axis=0, keepdims=True)
+                for top in range(g * padded, g * padded + columns, 8):
+                    part = first[top : top + 8, r * C : (r + 1) * C]
+                    plain = plain + part
+                    square = square + part * part
+            plain = jnp.sum(plain, axis=0, keepdims=True)
+            square = jnp.sum(square, axis=0, keepdims=True)
             sums.append(plain)
             squares.append(square)
         n = g1 - g0

time: 18.1 us -> 18.2 us (level)
  no operation moved by 1% of the time
where the time goes in v5:
time: 18.2 us; the launch traced here: 17.8 us
  Pallas kernels  8.39 us (46%)
  starting transfers between devices  5.25 us (29%)
  waiting for transfers between devices  4.11 us (23%)
    pallas_call x1, Pallas kernels, shards(): pl.pallas_call(functools.partial(body, cfg), out_shape=jax.ShapeDtypeStru...  4.81 us
    ppermute x1, starting transfers between devices, exchange_ring(): first = lax.ppermute(latents, axes, round_moves(FIRST_ROUND))  2.97 us
    ppermute x1, waiting for transfers between devices, exchange_ring(): third = lax.ppermute(held, axes, round_moves(SECOND_ROUND))  2.22 us
    ppermute x1, starting transfers between devices, exchange_ring(): third = lax.ppermute(held, axes, round_moves(SECOND_ROUND))  2.16 us
    ppermute x1, waiting for transfers between devices, exchange_ring(): first = lax.ppermute(latents, axes, round_moves(FIRST_ROUND))  1.89 us
    pallas_call x1, Pallas kernels, load_rest(): pl.pallas_call(functools.partial(load_body, rows), out_shape=pltpu.VMEM((...  1.86 us
    pallas_call x1, Pallas kernels, prepare(): pl.pallas_call(functools.partial(prepare_body, cfg), out_shape=(pltpu.VME...  1.72 us
  transfers between devices with their start and end apart: 4, of which 2 were waited for; matrix products, arithmetic and copies ran while one was open for 0% of the time, Pallas kernels for 20%

profile of v5, /device:TPU:0, one launch (start us, length us, event | category | flops | bytes accessed | tf_op | source)
XLA Modules:
  0.0 17.8 jit_solution(1179148958062580343)
XLA Ops:
  0.0 3.0 %collective-permute-start = (bf16[1,4,1664]{2,1,0:T(4,128)(2,1)}, bf16[1,4,1664]{2,1,0:T(4,128)(2,1)S(1)}, u32[]{:S(2)}, u32[]{:S(2)}) collective-permute-start(bf16[1,4,1664]{2,1,0:T(4,128)(2,1)} %bitcast.9), channel_id=1, source_target_pairs={{2,0},{0,2},{8,4},{10,6},{4,8},{6,10},{14,12},{12,14},{7,1},{5,3},... | collective-permute-start | bytes 39944 | tf_op jit(solution)/shard_map/ppermute | solution.py:97
  3.0 1.9 %collective-permute-done.refs_1_ = bf16[1,4,1664]{2,1,0:T(4,128)(2,1)S(1)} collective-permute-done((bf16[1,4,1664]{2,1,0:T(4,128)(2,1)}, bf16[1,4,1664]{2,1,0:T(4,128)(2,1)S(1)}, u32[]{:S(2)}, u32[]{:S(2)}) %collective-permute-start) | collective-permute-done | bytes 13344 | tf_op jit(solution)/shard_map/ppermute | solution.py:97
  4.9 0.0 collective-permute-start.1
  4.9 1.7 %shard_map.82 = (bf16[1,4,1664]{2,1,0:T(4,128)(2,1)S(1)}, bf16[384,768]{1,0:T(8,128)(2,1)S(1)}, bf16[384,384]{1,0:T(8,128)(2,1)S(1)}, f32[8,384]{1,0:T(8,128)S(1...) custom-call(bf16[1,4,1664]{2,1,0:T(4,128)(2,1)} %bitcast.10, ...), custom_call_target="tpu_custom_call" | custom-call | tf_op jit(solution)/shard_map/pallas_call | solution.py:255
  6.6 0.0 collective-permute-done.1.refs_2_
  6.6 2.2 %collective-permute-start.2 = (bf16[3,4,1664]{2,1,0:T(4,128)(2,1)S(1)}, bf16[3,4,1664]{2,1,0:T(4,128)(2,1)S(1)}, u32[]{:S(2)}, u32[]{:S(2)}) collective-permute-start(bf16[3,4,1664]{2,1,0:T(4,128)(2,1)S(1)} %shard_map.83), channel_id=1, source_target_pairs={{4,0},{6,2},{0,4},{2,6},{14,8},{12,10},{8,12},{10,14},{5,1},{7,3},... | collective-permute-start | bytes 119816 | tf_op jit(solution)/shard_map/ppermute | solution.py:100
  8.8 2.2 %collective-permute-done.2.refs_3_ = bf16[3,4,1664]{2,1,0:T(4,128)(2,1)S(1)} collective-permute-done((bf16[3,4,1664]{2,1,0:T(4,128)(2,1)S(1)}, bf16[3,4,1664]{2,1,0:T(4,128)(2,1)S(1)}, u32[]{:S(2)}, u32[]{:S(2)}) %collective-permute-start.2) | collective-permute-done | bytes 39968 | tf_op jit(solution)/shard_map/ppermute | solution.py:100
  11.0 0.1 collective-permute-start.3
  11.1 1.9 %shard_map.84.refs_11_ = bf16[2,3,576,384]{3,2,1,0:T(8,128)(2,1)S(1)} custom-call(bf16[3,3,576,384]{3,2,1,0:T(8,128)(2,1)} %bitcast.7), custom_call_target="tpu_custom_call" | custom-call | tf_op jit(solution)/shard_map/pallas_call | solution.py:299
  13.0 0.0 collective-permute-done.3.refs_4_
  13.0 4.8 %shard_map.85 = bf16[4,1,192,104]{3,2,1,0:T(8,128)(2,1)} custom-call(bf16[1,4,1664]{2,1,0:T(4,128)(2,1)S(1)} %get-tuple-element.12.refs_0_, bf16[1,4,1664]{2,1,0:T(4,128)(2,1)S(1)} %collective-permute-done.refs_1_, bf16[1,4,1664]{2,1,0:T(4,128)(2,1)S(1)} %collective-permute-done.1.refs_2_, bf16[3,4,1664]{2,1,0:T(4,128)(2,1)S(1)} %collective-permute-done.2.refs_3_, ...), custom_call_target="tpu_custom_call" | custom-call | tf_op jit(solution)/shard_map/pallas_call | solution.py:541
  (1 shorter events, 0.0 us)
Async XLA Ops:
  0.0 4.9 %collective-permute-start = (bf16[1,4,1664]{2,1,0:T(4,128)(2,1)}, bf16[1,4,1664]{2,1,0:T(4,128)(2,1)S(1)}, u32[]{:S(2)}, u32[]{:S(2)}) collective-permute-start(bf16[1,4,1664]{2,1,0:T(4,128)(2,1)} %bitcast.9), channel_id=1, source_target_pairs={{2,0},{0,2},{8,4},{10,6},{4,8},{6,10},{14,12},{12,14},{7,1},{5,3},... | collective-permute-start | bytes 39944 | tf_op jit(solution)/shard_map/ppermute | solution.py:97
  4.9 1.7 %collective-permute-start.1 = (bf16[1,4,1664]{2,1,0:T(4,128)(2,1)S(1)}, bf16[1,4,1664]{2,1,0:T(4,128)(2,1)S(1)}, u32[]{:S(2)}, u32[]{:S(2)}) collective-permute-start(bf16[1,4,1664]{2,1,0:T(4,128)(2,1)S(1)} %collective-permute-done.refs_1_), channel_id=1, source_target_pairs={{0,1},{1,0},{2,3},{3,2},{4,5},{5,4},{6,7},{7,6},{8,9},{9,8},{10,11... | collective-permute-start | bytes 39944 | tf_op jit(solution)/shard_map/ppermute | solution.py:98
  6.6 4.4 %collective-permute-start.2 = (bf16[3,4,1664]{2,1,0:T(4,128)(2,1)S(1)}, bf16[3,4,1664]{2,1,0:T(4,128)(2,1)S(1)}, u32[]{:S(2)}, u32[]{:S(2)}) collective-permute-start(bf16[3,4,1664]{2,1,0:T(4,128)(2,1)S(1)} %shard_map.83), channel_id=1, source_target_pairs={{4,0},{6,2},{0,4},{2,6},{14,8},{12,10},{8,12},{10,14},{5,1},{7,3},... | collective-permute-start | bytes 119816 | tf_op jit(solution)/shard_map/ppermute | solution.py:100
  11.0 2.0 %collective-permute-start.3 = (bf16[3,4,1664]{2,1,0:T(4,128)(2,1)S(1)}, bf16[3,4,1664]{2,1,0:T(4,128)(2,1)S(1)}, u32[]{:S(2)}, u32[]{:S(2)}) collective-permute-start(bf16[3,4,1664]{2,1,0:T(4,128)(2,1)S(1)} %collective-permute-done.2.refs_3_), channel_id=1, source_target_pairs={{0,1},{1,0},{2,3},{3,2},{4,5},{5,4},{6,7},{7,6},{8,9},{9,8},{10,11... | collective-permute-start | bytes 119816 | tf_op jit(solution)/shard_map/ppermute | solution.py:101
